TPU v7x, 32 devices: a whole 2x2x4 slice. The times are simulated.
32 devices in a mesh: fsdp: 8 (over y, x, core), tp: 4 (over z).
Axes of the slice: x: 2, y: 2, z: 4, core: 2. Of those that a mesh axis runs over, the one named last changes fastest.
Arguments:
- inputs: bfloat16 [2, 8, 1024, 2048], P(None, 'fsdp', 'tp'), may hold values from -6 to 6
- cotangent: bfloat16 [2, 8, 1024, 2048], P(None, 'fsdp', 'tp'), may hold values from -6 to 6
- segment_ids: int32 [2, 8, 1024], P(None, 'fsdp'), may hold values from 0 to 2, as said below
- block_ids: int32 [2, 8, 1024], P(None, 'fsdp'), may hold values from 0 to 1, as said below
- positions: int32 [2, 8, 1024], P(None, 'fsdp'), may hold values from 0 to 511, as said below
- w_qkv: bfloat16 [2048, 3, 2048], P('fsdp', None, 'tp'), may hold values from -0.15625 to 0.15625
- w_out: bfloat16 [2048, 2048], P('fsdp', 'tp'), may hold values from -0.75 to 0.75
- w_gateup: bfloat16 [2048, 2, 8192], P('fsdp', None, 'tp'), may hold values from -0.125 to 0.125
- w_down: bfloat16 [2048, 8192], P('fsdp', 'tp'), may hold values from -0.125 to 0.125
- gain_attn: bfloat16 [2048], P('fsdp'), may hold values from 0.25 to 1.75
- gain_ffn: bfloat16 [2048], P('fsdp'), may hold values from 0.25 to 1.75
Outputs:
- outputs: bfloat16 [2, 8, 1024, 2048], P(None, 'fsdp', 'tp')
- grad_inputs: float32 [2, 8, 1024, 2048], P(None, 'fsdp', 'tp')
- grad_qkv: float32 [2048, 3, 2048], P('fsdp', None, 'tp')
- grad_out: float32 [2048, 2048], P('fsdp', 'tp')
- grad_gateup: float32 [2048, 2, 8192], P('fsdp', None, 'tp')
- grad_down: float32 [2048, 8192], P('fsdp', 'tp')
- grad_gain_attn: float32 [2048], P('fsdp')
- grad_gain_ffn: float32 [2048], P('fsdp')
Inputs may be any that keep to these rules, and one draw needn't show every extreme that they name: `segment_ids`: each sequence holds 3 documents of one or more tokens, numbered in order from 0; the last one starts at token 512. `positions`: the token's offset from the first token of its document. `block_ids`: positions // 256.
All inputs are finite; a program needn't handle non-finite values.
Results may differ from a plain program's by a relative error of at most 0.015.
Values may be sent and summed in bfloat16 or wider, within the bound.
No kernel may reach another device: no remote copies, remote signals or barrier semaphores. Data moves between devices by JAX's collectives and lax.ppermute only.
A program may use at most 448 MiB of HBM per device.

v0:
```python
import math

import jax
import jax.numpy as jnp
from jax import lax
from jax.sharding import PartitionSpec as P

HD = 128


eps_norm = 1e-06
rope_base = 10000.0


def rope_tables(positions, half_size):
    ladder = jnp.arange(half_size, dtype=jnp.float32) * (1.0 / half_size)
    frequency = jnp.exp(-math.log(rope_base) * ladder)
    angles = positions.astype(jnp.float32)[:, None] * frequency[None, :]
    return (jnp.cos(angles)[:, None, :], jnp.sin(angles)[:, None, :])


def rotate(values, cosine, sine):
    half_size = values.shape[-1] // 2
    first_half = values[..., :half_size]
    second_half = values[..., half_size:]
    return jnp.concatenate(
        [first_half * cosine - second_half * sine, second_half * cosine + first_half * sine],
        axis=-1,
    )


def rotate_back(grads, cosine, sine):
    half_size = grads.shape[-1] // 2
    first_half = grads[..., :half_size]
    second_half = grads[..., half_size:]
    return jnp.concatenate(
        [first_half * cosine + second_half * sine, second_half * cosine - first_half * sine],
        axis=-1,
    )


def normalize(values):
    factor = lax.rsqrt(jnp.mean(values * values, axis=-1, keepdims=True) + eps_norm)
    return (values * factor, factor)


def normalize_back(grad_normed, unit, factor, gain):
    grad_unit = grad_normed * gain
    return factor * (grad_unit - unit * jnp.mean(grad_unit * unit, axis=-1, keepdims=True))


def visible(seg_query, blk_query, seg_keys, blk_keys):
    return (seg_query[:, None] == seg_keys[None, :]) & (blk_keys[None, :] <= blk_query[:, None])


def score_block(query_block, keys, shift):
    scale = 1.0 / math.sqrt(keys.shape[-1])
    return (
        jnp.einsum("qhd,khd->hqk", query_block, keys, preferred_element_type=jnp.float32) * scale
        + shift
    )


def attend(query, keys, values, seg_here, blk_here, shift):
    length, heads, size = query.shape
    block_rows = min(length, 512)
    blocks = length // block_rows
    query_blocks = query.reshape(blocks, block_rows, heads, size)
    seg_blocks = seg_here.reshape(blocks, block_rows)
    blk_blocks = blk_here.reshape(blocks, block_rows)

    def single_block(item):
        query_block, seg_block, blk_block = item
        scores = score_block(query_block, keys, shift)
        allowed = visible(seg_block, blk_block, seg_here, blk_here)
        weights = jnp.where(allowed[None], jax.nn.sigmoid(scores), 0.0).astype(jnp.bfloat16)
        return jnp.einsum("hqk,khd->qhd", weights, values, preferred_element_type=jnp.float32)

    mixed = lax.map(single_block, (query_blocks, seg_blocks, blk_blocks))
    return mixed.reshape(length, heads * size).astype(jnp.bfloat16)


def attend_back(query, keys, values, grad_mixed, seg_here, blk_here, shift):
    length, heads, size = query.shape
    scale = 1.0 / math.sqrt(size)
    block_rows = min(length, 512)
    blocks = length // block_rows
    query_blocks = query.reshape(blocks, block_rows, heads, size)
    grad_blocks = grad_mixed.reshape(blocks, block_rows, heads, size)
    seg_blocks = seg_here.reshape(blocks, block_rows)
    blk_blocks = blk_here.reshape(blocks, block_rows)

    def single_block(carry, item):
        grad_keys, grad_values = carry
        query_block, grad_block, seg_block, blk_block = item
        scores = score_block(query_block, keys, shift)
        allowed = visible(seg_block, blk_block, seg_here, blk_here)
        sigma = jax.nn.sigmoid(scores)
        weights = jnp.where(allowed[None], sigma, 0.0).astype(jnp.bfloat16)
        grad_weights = jnp.einsum(
            "qhd,khd->hqk", grad_block, values, preferred_element_type=jnp.float32
        )
        grad_scores = jnp.where(allowed[None], grad_weights * sigma * (1.0 - sigma), 0.0).astype(
            jnp.bfloat16
        )
        grad_values = grad_values + jnp.einsum(
            "hqk,qhd->khd", weights, grad_block, preferred_element_type=jnp.float32
        )
        grad_keys = (
            grad_keys
            + jnp.einsum(
                "hqk,qhd->khd", grad_scores, query_block, preferred_element_type=jnp.float32
            )
            * scale
        )
        grad_query = (
            jnp.einsum("hqk,khd->qhd", grad_scores, keys, preferred_element_type=jnp.float32)
            * scale
        )
        return ((grad_keys, grad_values), grad_query)

    zeros = jnp.zeros((length, heads, size), jnp.float32)
    (grad_keys, grad_values), grad_query = lax.scan(
        single_block, (zeros, zeros), (query_blocks, grad_blocks, seg_blocks, blk_blocks)
    )
    return (grad_query.reshape(length, heads, size), grad_keys, grad_values)


def grad_rows(saved, count):
    total = None
    for (
        normed_full,
        grad_qkv,
        grad_middle_full,
        mixed,
        normed_two_full,
        grad_gu,
        grad_top_full,
        hidden,
    ) in saved:
        term_qkv = jnp.einsum(
            "td,tce->dce", normed_full, grad_qkv, preferred_element_type=jnp.float32
        ).reshape(count, -1)
        term_out = jnp.einsum(
            "td,tc->dc", grad_middle_full, mixed, preferred_element_type=jnp.float32
        )
        term_gu = jnp.einsum(
            "td,tce->dce", normed_two_full, grad_gu, preferred_element_type=jnp.float32
        ).reshape(count, -1)
        term_down = jnp.einsum(
            "td,tf->df", grad_top_full, hidden, preferred_element_type=jnp.float32
        )
        joined = jnp.concatenate([term_qkv, term_out, term_gu, term_down], axis=1)
        total = joined
    return total


def local(
    inputs,
    cotangent,
    segment_ids,
    block_ids,
    positions,
    w_qkv,
    w_out,
    w_gateup,
    w_down,
    gain_attn,
    gain_ffn,
):
    micro = inputs.shape[0]
    local_rows = inputs.shape[2]
    width = inputs.shape[3]
    length = segment_ids.shape[2]
    shard_rows = w_qkv.shape[0]
    width_here = w_qkv.shape[2]
    hidden_here = w_gateup.shape[2]
    heads_here = width_here // HD
    shift = -math.log(length)
    results = []
    grad_results = []
    summed = None
    gain_one_total = jnp.zeros((width,), jnp.float32)
    gain_two_total = jnp.zeros((width,), jnp.float32)
    for batch_index in range(micro):
        qkv_full, out_full, gain_one = (
            lax.all_gather(w_qkv, "fsdp", axis=0, tiled=True),
            lax.all_gather(w_out, "fsdp", axis=0, tiled=True),
            lax.all_gather(gain_attn, "fsdp", axis=0, tiled=True),
        )
        gateup_full, down_full, gain_two = (
            lax.all_gather(w_gateup, "fsdp", axis=0, tiled=True),
            lax.all_gather(w_down, "fsdp", axis=0, tiled=True),
            lax.all_gather(gain_ffn, "fsdp", axis=0, tiled=True),
        )
        gain_one = gain_one.astype(jnp.float32)
        gain_two = gain_two.astype(jnp.float32)
        seg_here = segment_ids[batch_index, 0]
        blk_here = block_ids[batch_index, 0]
        cosine, sine = rope_tables(positions[batch_index, 0], HD // 2)
        residual = inputs[batch_index, 0].astype(jnp.float32)
        unit_one, factor_one = normalize(residual)
        normed_one = (unit_one * gain_one).astype(jnp.bfloat16)
        normed_full = lax.all_gather(normed_one, "tp", axis=0, tiled=True)
        projected = jnp.einsum(
            "td,dce->tce", normed_full, qkv_full, preferred_element_type=jnp.float32
        )
        query = rotate(projected[:, 0].reshape(length, heads_here, HD), cosine, sine).astype(
            jnp.bfloat16
        )
        keys = rotate(projected[:, 1].reshape(length, heads_here, HD), cosine, sine).astype(
            jnp.bfloat16
        )
        values = projected[:, 2].reshape(length, heads_here, HD).astype(jnp.bfloat16)
        mixed = attend(query, keys, values, seg_here, blk_here, shift)

        def attn_term(start, count, mixed=mixed, out_full=out_full):
            return jnp.einsum("tc,dc->td", mixed, out_full, preferred_element_type=jnp.float32)

        middle = residual + lax.psum_scatter(
            attn_term(jnp.int32(0), local_rows * lax.axis_size("tp")),
            "tp",
            scatter_dimension=0,
            tiled=True,
        )
        unit_two, factor_two = normalize(middle)
        normed_two = (unit_two * gain_two).astype(jnp.bfloat16)
        normed_two_full = lax.all_gather(normed_two, "tp", axis=0, tiled=True)
        gate_up = jnp.einsum(
            "td,dce->tce", normed_two_full, gateup_full, preferred_element_type=jnp.float32
        )
        gate = gate_up[:, 0]
        up_part = gate_up[:, 1]
        gate_sigma = jax.nn.sigmoid(gate)
        gate_silu = gate * gate_sigma
        hidden = (gate_silu * up_part).astype(jnp.bfloat16)

        def ffn_term(start, count, hidden=hidden, down_full=down_full):
            return jnp.einsum("tf,df->td", hidden, down_full, preferred_element_type=jnp.float32)

        results.append(
            (
                middle
                + lax.psum_scatter(
                    ffn_term(jnp.int32(0), local_rows * lax.axis_size("tp")),
                    "tp",
                    scatter_dimension=0,
                    tiled=True,
                )
            ).astype(jnp.bfloat16)
        )
        grad_top = cotangent[batch_index, 0]
        grad_top_full = lax.all_gather(grad_top, "tp", axis=0, tiled=True)
        grad_hidden = jnp.einsum(
            "td,df->tf", grad_top_full, down_full, preferred_element_type=jnp.float32
        )
        grad_gate = grad_hidden * up_part * gate_sigma * (1.0 + gate * (1.0 - gate_sigma))
        grad_up = grad_hidden * gate_silu
        grad_gu = jnp.stack([grad_gate, grad_up], axis=1).astype(jnp.bfloat16)

        def ffn_back_term(start, count, grad_gu=grad_gu, gateup_full=gateup_full):
            return jnp.einsum(
                "tce,dce->td", grad_gu, gateup_full, preferred_element_type=jnp.float32
            )

        grad_normed_two = lax.psum_scatter(
            ffn_back_term(jnp.int32(0), local_rows * lax.axis_size("tp")),
            "tp",
            scatter_dimension=0,
            tiled=True,
        )
        grad_middle = grad_top.astype(jnp.float32) + normalize_back(
            grad_normed_two, unit_two, factor_two, gain_two
        )
        gain_two_total = gain_two_total + jnp.sum(grad_normed_two * unit_two, axis=0)
        grad_middle_full = lax.all_gather(
            grad_middle.astype(jnp.bfloat16), "tp", axis=0, tiled=True
        )
        grad_mixed = jnp.einsum(
            "td,dc->tc", grad_middle_full, out_full, preferred_element_type=jnp.float32
        ).astype(jnp.bfloat16)
        grad_query, grad_keys, grad_values = attend_back(
            query,
            keys,
            values,
            grad_mixed.reshape(length, heads_here, HD),
            seg_here,
            blk_here,
            shift,
        )
        grad_qkv = jnp.stack(
            [
                rotate_back(grad_query, cosine, sine).reshape(length, width_here),
                rotate_back(grad_keys, cosine, sine).reshape(length, width_here),
                grad_values.reshape(length, width_here),
            ],
            axis=1,
        ).astype(jnp.bfloat16)

        def attn_back_term(start, count, grad_qkv=grad_qkv, qkv_full=qkv_full):
            return jnp.einsum("tce,dce->td", grad_qkv, qkv_full, preferred_element_type=jnp.float32)

        grad_normed_one = lax.psum_scatter(
            attn_back_term(jnp.int32(0), local_rows * lax.axis_size("tp")),
            "tp",
            scatter_dimension=0,
            tiled=True,
        )
        grad_results.append(
            grad_middle + normalize_back(grad_normed_one, unit_one, factor_one, gain_one)
        )
        gain_one_total = gain_one_total + jnp.sum(grad_normed_one * unit_one, axis=0)
        record = (
            normed_full,
            grad_qkv,
            grad_middle_full,
            mixed,
            normed_two_full,
            grad_gu,
            grad_top_full,
            hidden,
        )
        batch_sum = lax.psum_scatter(
            grad_rows([record], shard_rows * lax.axis_size("fsdp")),
            "fsdp",
            scatter_dimension=0,
            tiled=True,
        )
        summed = batch_sum if summed is None else summed + batch_sum
    edge_one = 3 * width_here
    edge_two = 4 * width_here
    edge_three = edge_two + 2 * hidden_here
    grad_qkv_rows = summed[:, :edge_one].reshape(shard_rows, 3, width_here)
    grad_out_rows = summed[:, edge_one:edge_two]
    grad_gateup_rows = summed[:, edge_two:edge_three].reshape(shard_rows, 2, hidden_here)
    grad_down_rows = summed[:, edge_three:]
    gain_totals = lax.psum((gain_one_total, gain_two_total), ("fsdp", "tp"))
    first_row = lax.axis_index("fsdp") * shard_rows
    grad_gain_one = lax.dynamic_slice_in_dim(gain_totals[0], first_row, shard_rows, 0)
    grad_gain_two = lax.dynamic_slice_in_dim(gain_totals[1], first_row, shard_rows, 0)
    outputs = jnp.stack(results)[:, None]
    grad_inputs = jnp.stack(grad_results)[:, None]
    return (
        outputs,
        grad_inputs,
        grad_qkv_rows,
        grad_out_rows,
        grad_gateup_rows,
        grad_down_rows,
        grad_gain_one,
        grad_gain_two,
    )


def solution(mesh):
    return jax.shard_map(
        local,
        mesh=mesh,
        in_specs=(
            P(None, "fsdp", "tp", None),
            P(None, "fsdp", "tp", None),
            P(None, "fsdp", None),
            P(None, "fsdp", None),
            P(None, "fsdp", None),
            P("fsdp", None, "tp"),
            P("fsdp", "tp"),
            P("fsdp", None, "tp"),
            P("fsdp", "tp"),
            P("fsdp"),
            P("fsdp"),
        ),
        out_specs=(
            P(None, "fsdp", "tp", None),
            P(None, "fsdp", "tp", None),
            P("fsdp", None, "tp"),
            P("fsdp", "tp"),
            P("fsdp", None, "tp"),
            P("fsdp", "tp"),
            P("fsdp"),
            P("fsdp"),
        ),
        check_vma=False,
    )
```

profile of v0, /device:TPU:0, one launch (start us, length us, event | category | flops | bytes accessed | tf_op | source)
XLA Modules:
  0.0 2625.4 jit_solution(9029248649873749477)
XLA Ops:
  10.1 10.6 all-gather.2
  25.4 5.0 multiply_cosine_fusion.1
  30.4 73.5 %all-gather.29.cloned.1.call-done = bf16[1024,2048]{1,0:T(8,128)(2,1)} async-done(((bf16[256,2048]{1,0:T(8,128)(2,1)}), bf16[1024,2048]{1,0:T(8,128)(2,1)}) %all-gather.29.cloned.1.call-update) | async-done | bytes 4194320 | tf_op jit(solution)/shard_map/all_gather | solution.py:204
  103.8 47.6 %all-gather.19.cloned.1.call-done = bf16[2048,3,512]{0,2,1:T(8,128)(2,1)} async-done(((bf16[256,3,512]{0,2,1:T(8,128)(2,1)}), bf16[2048,3,512]{0,2,1:T(8,128)(2,1)}) %all-gather.19.cloned.1.call-update) | async-done | bytes 6291472 | tf_op jit(solution)/shard_map/all_gather | solution.py:187
  151.4 10.1 fusion.75
  178.3 56.0 %all-gather.17.cloned.1.call-done = bf16[1024,2048]{1,0:T(8,128)(2,1)} async-done(((bf16[256,2048]{1,0:T(8,128)(2,1)}), bf16[1024,2048]{1,0:T(8,128)(2,1)}) %all-gather.17.cloned.1.call-update) | async-done | bytes 4194320 | tf_op jit(solution)/shard_map/all_gather | solution.py:204
  234.3 10.1 fusion.82
  262.6 8.9 subtract_convert_fusion.4
  281.0 12.1 while.50
  281.5 5.6 fusion.212
  287.5 5.6 fusion.212
  296.9 7.6 fusion.118
  312.5 12.1 while.51
  313.0 5.6 fusion.216
  319.1 5.6 fusion.216
  328.4 7.2 fusion.114
  339.8 8.9 all-gather.3
  348.7 99.1 %reduce-scatter.10.cloned.1.call-done = f32[256,2048]{1,0:T(8,128)} async-done(((f32[1024,2048]{1,0:T(8,128)}), f32[256,2048]{1,0:T(8,128)}) %reduce-scatter.10.cloned.1.call-update) | async-done | bytes 2097168 | tf_op jit(solution)/shard_map/reduce_scatter | solution.py:220
  447.9 147.5 %reduce-scatter.14.cloned.1.call-done = f32[256,2048]{1,0:T(8,128)} async-done(((f32[1024,2048]{1,0:T(8,128)}), f32[256,2048]{1,0:T(8,128)}) %reduce-scatter.14.cloned.1.call-update) | async-done | bytes 2097168 | tf_op jit(solution)/shard_map/reduce_scatter | solution.py:220
  595.3 4.1 multiply_reduce_fusion.5
  604.2 84.0 %all-gather.25.cloned.1.call-done = bf16[2048,2,2048]{2,0,1:T(8,128)(2,1)} async-done(((bf16[256,2,2048]{2,0,1:T(8,128)(2,1)}), bf16[2048,2,2048]{2,0,1:T(8,128)(2,1)}) %all-gather.25.cloned.1.call-update) | async-done | bytes 16777232 | tf_op jit(solution)/shard_map/all_gather | solution.py:192
  688.2 82.9 %all-gather.23.cloned.1.call-done = bf16[1024,2048]{1,0:T(8,128)(2,1)} async-done(((bf16[256,2048]{1,0:T(8,128)(2,1)}), bf16[1024,2048]{1,0:T(8,128)(2,1)}) %all-gather.23.cloned.1.call-update) | async-done | bytes 4194320 | tf_op jit(solution)/shard_map/all_gather | solution.py:228
  771.1 23.6 fusion.78
  794.7 57.8 %all-gather.37.cloned.1.call-done = bf16[1,1,1024,2048]{3,2,1,0:T(8,128)(2,1)} async-done(((bf16[1,1,256,2048]{3,2,1,0:T(8,128)(2,1)}), bf16[1,1,1024,2048]{3,2,1,0:T(8,128)(2,1)}) %all-gather.37.cloned.1.call-update) | async-done | bytes 4194320 | tf_op jit(solution)/shard_map/all_gather | solution.py:253
  852.5 54.5 %all-gather.27.cloned.1.call-done = bf16[2048,2048]{1,0:T(8,128)(2,1)} async-done(((bf16[256,2048]{1,0:T(8,128)(2,1)}), bf16[2048,2048]{1,0:T(8,128)(2,1)}) %all-gather.27.cloned.1.call-update) | async-done | bytes 8388624 | tf_op jit(solution)/shard_map/all_gather | solution.py:193
  907.0 20.9 fusion.84
  929.9 23.0 fusion.60
  953.1 144.7 %reduce-scatter.18.cloned.1.call-done = f32[256,2048]{1,0:T(8,128)} async-done(((f32[1024,2048]{1,0:T(8,128)}), f32[256,2048]{1,0:T(8,128)}) %reduce-scatter.18.cloned.1.call-update) | async-done | bytes 2097168 | tf_op jit(solution)/shard_map/reduce_scatter | solution.py:266
  1097.8 4.5 multiply_reduce_fusion.1
  1103.0 80.7 %all-gather.31.cloned.1.call-done = bf16[1024,2048]{1,0:T(8,128)(2,1)} async-done(((bf16[256,2048]{1,0:T(8,128)(2,1)}), bf16[1024,2048]{1,0:T(8,128)(2,1)}) %all-gather.31.cloned.1.call-update) | async-done | bytes 4194320 | tf_op jit(solution)/shard_map/all_gather | solution.py:228
  1183.7 23.6 fusion.71
  1207.4 57.2 %all-gather.39.cloned.1.call-done = bf16[1,1,1024,2048]{3,2,1,0:T(8,128)(2,1)} async-done(((bf16[1,1,256,2048]{3,2,1,0:T(8,128)(2,1)}), bf16[1,1,1024,2048]{3,2,1,0:T(8,128)(2,1)}) %all-gather.39.cloned.1.call-update) | async-done | bytes 4194320 | tf_op jit(solution)/shard_map/all_gather | solution.py:253
  1264.6 20.9 fusion.85
  1287.4 23.0 fusion.61
  1310.5 15.0 fusion.146
  1325.6 128.2 %reduce-scatter.22.cloned.1.call-done = f32[256,2048]{1,0:T(8,128)} async-done(((f32[1024,2048]{1,0:T(8,128)}), f32[256,2048]{1,0:T(8,128)}) %reduce-scatter.22.cloned.1.call-update) | async-done | bytes 2097168 | tf_op jit(solution)/shard_map/reduce_scatter | solution.py:266
  1456.5 144.7 %reduce-scatter.16.cloned.1.call-done = f32[256,2048]{1,0:T(8,128)} async-done(((f32[1024,2048]{1,0:T(8,128)}), f32[256,2048]{1,0:T(8,128)}) %reduce-scatter.16.cloned.1.call-update) | async-done | bytes 2097168 | tf_op jit(solution)/shard_map/reduce_scatter | solution.py:244
  1601.2 5.8 fusion.132
  1607.7 80.9 %all-gather.35.cloned.1.call-done = bf16[1024,2048]{1,0:T(8,128)(2,1)} async-done(((bf16[256,2048]{1,0:T(8,128)(2,1)}), bf16[1024,2048]{1,0:T(8,128)(2,1)}) %all-gather.35.cloned.1.call-update) | async-done | bytes 4194320 | tf_op jit(solution)/shard_map/all_gather | solution.py:276
  1688.6 6.2 convolution_convert_fusion
  1698.9 28.3 %while.53 = (s32[]{:T(128)}, f32[1024,4,128]{0,2,1:T(8,128)S(1)}, f32[1024,4,128]{0,2,1:T(8,128)}, f32[2,512,4,128]{3,1,0,2:T(8,128)}, bf16[2,512,4,128]{3,1,2,0...) while((s32[]{:T(128)}, f32[1024,4,128]{0,2,1:T(8,128)S(1)}, ...), condition=%wide.region_21.22_spmd.clone, body=%wide.region_20.21_spmd.clone.sunk | while | flops 2711879680 | bytes 97014096 | solution.py:123
  1734.2 5.9 add_convert_fusion.1
  1745.7 11.0 convolution_bitcast_fusion.2
  1756.8 13.0 all-gather.33.cloned.1.call-done
  1769.8 6.2 convolution_convert_fusion.1
  1780.1 28.4 %while.52 = (s32[]{:T(128)}, f32[1024,4,128]{0,2,1:T(8,128)S(1)}, f32[1024,4,128]{0,2,1:T(8,128)}, f32[2,512,4,128]{3,1,0,2:T(8,128)}, bf16[2,512,4,128]{3,1,2,0...) while((s32[]{:T(128)}, f32[1024,4,128]{0,2,1:T(8,128)S(1)}, ...), condition=%wide.region_15.16_spmd.clone, body=%wide.region_14.15_spmd.clone.sunk | while | flops 2711879680 | bytes 97014096 | solution.py:123
  1796.0 4.0 add_divide_fusion.6
  1815.3 6.0 add_convert_fusion.3
  1827.0 11.0 convolution_bitcast_fusion.3
  1838.1 14.6 fusion.145
  1852.8 25.6 fusion.58
  1878.4 14.3 convolution_bitcast_fusion.1
  1892.7 11.9 convolution_bitcast_fusion
  1904.6 23.5 fusion.56
  1933.8 9.8 fusion.73
  1943.6 9.9 fusion.80
  1953.5 64.7 %maximum_add_fusion = f32[2048,8192]{0,1:T(8,128)} fusion(f32[2048,2048]{0,1:T(8,128)} %convolution_bitcast_fusion.1, f32[2048,4096]{0,1:T(8,128)} %bitcast.392, f32[2048,512]{0,1:T(8,128)S(1)} %fusion.116, f32[2048,1536]{0,1:T(8,128)} %bitcast.398, f32[2048,2048]{0,1:T(8,128)} %convolution_bitcast_fusion, f32[2048,4096]{0,1:T(8,128)} %bitcast.393, ...), kind=kLoop, calls=%fused_computation.76 | loop fusion | flops 117440512 | bytes 201326592 | tf_op jit(solution)/shard_map/add | solution.py:329
  2019.0 43.8 %reduce-scatter.20.cloned.1.call-done = f32[256,2048]{1,0:T(8,128)} async-done(((f32[1024,2048]{1,0:T(8,128)}), f32[256,2048]{1,0:T(8,128)}) %reduce-scatter.20.cloned.1.call-update) | async-done | bytes 2097168 | tf_op jit(solution)/shard_map/reduce_scatter | solution.py:303
  2066.1 45.9 %all-reduce = (f32[2048]{0:T(1024)S(1)}, f32[2048]{0:T(1024)S(1)}) all-reduce(f32[2048]{0:T(1024)S(1)} %add.202, f32[2048]{0:T(1024)S(1)} %add.204), channel_id=1, replica_groups=mesh['fsdp'=8,'tp'=4] {'fsdp','tp'}, use_global_device_ids=true, to_apply=%region_28.29 | all-reduce | flops 4096 | bytes 32768 | tf_op jit(solution)/shard_map/psum | solution.py:337
  2113.3 97.9 %reduce-scatter.12.cloned.1.call-done = f32[256,2048]{1,0:T(8,128)} async-done(((f32[1024,2048]{1,0:T(8,128)}), f32[256,2048]{1,0:T(8,128)}) %reduce-scatter.12.cloned.1.call-update) | async-done | bytes 2097168 | tf_op jit(solution)/shard_map/reduce_scatter | solution.py:244
  2211.2 5.2 fusion.99
  2223.0 376.2 %reduce-scatter.26.cloned.1.call-done = f32[256,8192]{0,1:T(8,128)} async-done(((f32[2048,8192]{0,1:T(8,128)}), f32[256,8192]{0,1:T(8,128)}) %reduce-scatter.26.cloned.1.call-update) | async-done | bytes 8388624 | tf_op jit(solution)/shard_map/reduce_scatter | solution.py:323
  2603.0 4.5 slice.190
  2607.4 7.3 copy.165
  (409 shorter events, 196.7 us)
Async XLA Ops:
  7.2 13.5 copy-start.4
  7.2 96.7 %all-gather.29.cloned.1.call-start = ((), (), s32[]{:S(2)}) async-start(), calls=%async_computation.17 | async-start | bytes 5242880 | tf_op jit(solution)/shard_map/all_gather | solution.py:204
  10.0 12.6 copy-start.53
  10.1 12.5 copy-start.82
  10.1 12.5 copy-start.80
  22.6 128.7 %all-gather.19.cloned.1.call-start = ((), (), s32[]{:S(2)}) async-start(), calls=%async_computation.10 | async-start | bytes 7077888 | tf_op jit(solution)/shard_map/all_gather | solution.py:187
  23.9 210.4 %all-gather.17.cloned.1.call-start = ((), (), s32[]{:S(2)}) async-start(), calls=%async_computation.9 | async-start | bytes 5242880 | tf_op jit(solution)/shard_map/all_gather | solution.py:204
  24.6 272.3 %all-gather.21.cloned.1.call-start = ((), (), s32[]{:S(2)}) async-start(), calls=%async_computation.11 | async-start | bytes 2359296 | tf_op jit(solution)/shard_map/all_gather | solution.py:188
  25.2 422.7 %reduce-scatter.10.cloned.1.call-start = ((), (), s32[]{:S(2)}) async-start(), calls=%async_computation.12 | async-start | bytes 10485760 | tf_op jit(solution)/shard_map/reduce_scatter | solution.py:220
  30.4 232.3 %copy-start.26 = (f32[1024,64]{1,0:T(8,128)}, f32[1024,64]{1,0:T(8,128)S(1)}, u32[]{:S(2)}) copy-start(f32[1024,64]{1,0:T(8,128)S(1)} %get-tuple-element.640) | copy-start | bytes 786436
  30.4 232.3 %copy-start.28 = (f32[1024,64]{1,0:T(8,128)}, f32[1024,64]{1,0:T(8,128)S(1)}, u32[]{:S(2)}) copy-start(f32[1024,64]{1,0:T(8,128)S(1)} %get-tuple-element.641) | copy-start | bytes 786436
  293.1 11.4 copy-start.10
  293.1 11.4 copy-start.21
  293.1 11.4 copy-start.54
  293.1 11.4 copy-start.56
  293.1 11.4 copy-start.66
  293.1 11.4 copy-start.68
  304.6 290.7 %reduce-scatter.14.cloned.1.call-start = ((), (), s32[]{:S(2)}) async-start(), calls=%async_computation.18 | async-start | bytes 10485760 | tf_op jit(solution)/shard_map/reduce_scatter | solution.py:220
  324.6 11.1 copy-start.12
  324.6 11.1 copy-start.23
  324.6 11.1 copy-start.58
  324.6 11.1 copy-start.60
  324.6 11.1 copy-start.70
  324.6 11.1 copy-start.72
  335.7 259.6 %copy-start.5 = (bf16[2,1,256,2048]{3,2,1,0:T(8,128)(2,1)S(1)}, bf16[2,1,256,2048]{3,2,1,0:T(8,128)(2,1)}, u32[]{:S(2)}) copy-start(bf16[2,1,256,2048]{3,2,1,0:T(8,128)(2,1)} %param.19) | copy-start | bytes 6291460
  335.8 352.4 %all-gather.25.cloned.1.call-start = ((), (), s32[]{:S(2)}) async-start(), calls=%async_computation.14 | async-start | bytes 18874368 | tf_op jit(solution)/shard_map/all_gather | solution.py:192
  339.8 431.3 %all-gather.23.cloned.1.call-start = ((), (), s32[]{:S(2)}) async-start(), calls=%async_computation.13 | async-start | bytes 5242880 | tf_op jit(solution)/shard_map/all_gather | solution.py:228
  348.7 1252.5 %copy-start.62 = (f32[8,1,256]{2,1,0:T(1,128)}, f32[8,1,256]{2,1,0:T(1,128)S(1)}, u32[]{:S(2)}) copy-start(f32[8,1,256]{2,1,0:T(1,128)S(1)} %convert_element_type.165) | copy-start | bytes 24580
  599.4 1001.8 %copy-start.76 = (f32[256]{0:T(256)}, f32[256]{0:T(256)S(1)}, u32[]{:S(2)}) copy-start(f32[256]{0:T(256)S(1)} %add_rsqrt_fusion.2) | copy-start | bytes 3076
  602.0 250.5 %all-gather.37.cloned.1.call-start = ((), (), s32[]{:S(2)}) async-start(), calls=%async_computation.27 | async-start | bytes 5242880 | tf_op jit(solution)/shard_map/all_gather | solution.py:253
  603.5 303.5 %all-gather.27.cloned.1.call-start = ((), (), s32[]{:S(2)}) async-start(), calls=%async_computation.15 | async-start | bytes 9437184 | tf_op jit(solution)/shard_map/all_gather | solution.py:193
  604.1 493.6 %reduce-scatter.18.cloned.1.call-start = ((), (), s32[]{:S(2)}) async-start(), calls=%async_computation.21 | async-start | bytes 10485760 | tf_op jit(solution)/shard_map/reduce_scatter | solution.py:266
  953.0 144.8 %copy-start.7 = (f32[256,2048]{1,0:T(8,128)S(1)}, f32[256,2048]{1,0:T(8,128)}, u32[]{:S(2)}) copy-start(f32[256,2048]{1,0:T(8,128)} %get-tuple-element.616) | copy-start | bytes 6291460
  953.0 230.8 %all-gather.31.cloned.1.call-start = ((), (), s32[]{:S(2)}) async-start(), calls=%async_computation.19 | async-start | bytes 5242880 | tf_op jit(solution)/shard_map/all_gather | solution.py:228
  953.0 648.2 %copy-start.78 = (f32[256]{0:T(256)}, f32[256]{0:T(256)S(1)}, u32[]{:S(2)}) copy-start(f32[256]{0:T(256)S(1)} %add_rsqrt_fusion) | copy-start | bytes 3076
  1102.2 162.3 %all-gather.39.cloned.1.call-start = ((), (), s32[]{:S(2)}) async-start(), calls=%async_computation.28 | async-start | bytes 5242880 | tf_op jit(solution)/shard_map/all_gather | solution.py:253
  1103.0 350.8 %reduce-scatter.22.cloned.1.call-start = ((), (), s32[]{:S(2)}) async-start(), calls=%async_computation.24 | async-start | bytes 10485760 | tf_op jit(solution)/shard_map/reduce_scatter | solution.py:266
  1310.5 290.8 %reduce-scatter.16.cloned.1.call-start = ((), (), s32[]{:S(2)}) async-start(), calls=%async_computation.20 | async-start | bytes 10485760 | tf_op jit(solution)/shard_map/reduce_scatter | solution.py:244
  1325.5 363.0 %all-gather.35.cloned.1.call-start = ((), (), s32[]{:S(2)}) async-start(), calls=%async_computation.25 | async-start | bytes 5242880 | tf_op jit(solution)/shard_map/all_gather | solution.py:276
  1325.6 281.4 %copy-start.86 = (f32[256]{0:T(256)}, f32[256]{0:T(256)S(1)}, u32[]{:S(2)}) copy-start(f32[256]{0:T(256)S(1)} %broadcast_multiply_fusion.3) | copy-start | bytes 3076
  1456.5 150.5 %copy-start.84 = (f32[256]{0:T(256)}, f32[256]{0:T(256)S(1)}, u32[]{:S(2)}) copy-start(f32[256]{0:T(256)S(1)} %broadcast_multiply_fusion.1) | copy-start | bytes 3076
  1607.1 162.7 %all-gather.33.cloned.1.call-start = ((), (), s32[]{:S(2)}) async-start(), calls=%async_computation.22 | async-start | bytes 5242880 | tf_op jit(solution)/shard_map/all_gather | solution.py:276
  1607.7 411.3 %reduce-scatter.24.cloned.1.call-start = ((), (), s32[]{:S(2)}) async-start(), calls=%async_computation.26 | async-start | bytes 10485760 | tf_op jit(solution)/shard_map/reduce_scatter | solution.py:303
  1756.7 306.1 %reduce-scatter.20.cloned.1.call-start = ((), (), s32[]{:S(2)}) async-start(), calls=%async_computation.23 | async-start | bytes 10485760 | tf_op jit(solution)/shard_map/reduce_scatter | solution.py:303
  1838.0 373.2 %reduce-scatter.12.cloned.1.call-start = ((), (), s32[]{:S(2)}) async-start(), calls=%async_computation.16 | async-start | bytes 10485760 | tf_op jit(solution)/shard_map/reduce_scatter | solution.py:244
  1852.7 746.4 %reduce-scatter.26.cloned.1.call-start = ((), (), s32[]{:S(2)}) async-start(), calls=%async_computation.29 | async-start | bytes 75497472 | tf_op jit(solution)/shard_map/reduce_scatter | solution.py:323
  1852.8 25.6 copy-start.93
  1878.4 14.3 copy-start.95
  1878.4 14.3 copy-start.99
  1892.7 11.9 copy-start.94
  1904.6 23.5 copy-start.42
  1904.6 23.5 copy-start.97
  1933.8 9.8 copy-start.52
  1933.8 9.8 copy-start.92
  2018.3 44.5 %copy-start.6 = (bf16[2,1,256,2048]{3,2,1,0:T(8,128)(2,1)S(1)}, bf16[2,1,256,2048]{3,2,1,0:T(8,128)(2,1)}, u32[]{:S(2)}) copy-start(bf16[2,1,256,2048]{3,2,1,0:T(8,128)(2,1)} %param.19) | copy-start | bytes 6291460
  2018.3 44.5 %copy-start.65 = (f32[8,1,256]{2,1,0:T(1,128)S(1)}, f32[8,1,256]{2,1,0:T(1,128)}, u32[]{:S(2)}) copy-start(f32[8,1,256]{2,1,0:T(1,128)} %copy-done.64) | copy-start | bytes 24580
  2018.3 44.5 %copy-start.81 = (f32[256]{0:T(256)S(1)}, f32[256]{0:T(256)}, u32[]{:S(2)}) copy-start(f32[256]{0:T(256)} %copy-done.80) | copy-start | bytes 3076
  2018.3 44.5 %copy-start.83 = (f32[256]{0:T(256)S(1)}, f32[256]{0:T(256)}, u32[]{:S(2)}) copy-start(f32[256]{0:T(256)} %copy-done.82) | copy-start | bytes 3076
  2019.0 192.2 %copy-start.63 = (f32[8,1,256]{2,1,0:T(1,128)S(1)}, f32[8,1,256]{2,1,0:T(1,128)}, u32[]{:S(2)}) copy-start(f32[8,1,256]{2,1,0:T(1,128)} %copy-done.62) | copy-start | bytes 24580
  2019.0 192.2 %copy-start.77 = (f32[256]{0:T(256)S(1)}, f32[256]{0:T(256)}, u32[]{:S(2)}) copy-start(f32[256]{0:T(256)} %copy-done.76) | copy-start | bytes 3076
  2019.0 192.2 %copy-start.87 = (f32[256]{0:T(256)S(1)}, f32[256]{0:T(256)}, u32[]{:S(2)}) copy-start(f32[256]{0:T(256)} %copy-done.86) | copy-start | bytes 3076
  2113.3 103.2 %copy-start.34 = (bf16[1,256,2048]{2,1,0:T(8,128)(2,1)S(1)}, bf16[1,256,2048]{2,1,0:T(8,128)(2,1)}, u32[]{:S(2)}) copy-start(bf16[1,256,2048]{2,1,0:T(8,128)(2,1)} %get-tuple-element.610) | copy-start | bytes 3145732
  2211.2 6.8 copy-start.16
  2211.2 6.8 copy-start.25
  (73 other events, 194.7 us)
Sparse Core Ops, SparseCore 0:
  22.8 81.0 all-gather.28
  106.3 45.0 all-gather.18
  153.5 80.7 all-gather.16
  236.0 26.2 all-gather.20
  304.7 143.0 reduce-scatter.9
  450.1 145.2 reduce-scatter.13
  597.8 90.3 all-gather.24
  690.3 80.7 all-gather.22
  773.2 79.2 all-gather.36
  854.2 52.7 all-gather.26
  953.1 144.6 reduce-scatter.17
  1102.4 81.3 all-gather.30
  1185.3 79.2 all-gather.38
  1310.6 143.0 reduce-scatter.21
  1455.9 145.2 reduce-scatter.15
  1607.2 81.3 all-gather.34
  1690.5 79.2 all-gather.32
  1772.0 143.0 reduce-scatter.23
  1917.5 145.2 reduce-scatter.19
  2065.0 146.1 reduce-scatter.11
  2214.8 384.3 reduce-scatter.25
where the time goes:
time: 2640 us; the launch traced here: 2630 us
  waiting for transfers between devices  1870 us (71%)
  matrix products  398 us (15%)
  other arithmetic  146 us (6%)
  local copies, waits for them, and re-layouts  125 us (5%)
  blocking collectives  65.3 us (2%)
    reduce_scatter x1, waiting for transfers between devices, local(): lax.psum_scatter(grad_rows([record], shard_rows * lax.axis_size('fsdp')),...  376 us
    reduce_scatter x2, waiting for transfers between devices, local(): lax.psum_scatter(ffn_back_term(jnp.int32(0), local_rows * lax.axis_size('...  273 us
    reduce_scatter x2, waiting for transfers between devices, local(): lax.psum_scatter(attn_term(jnp.int32(0), local_rows * lax.axis_size('tp')...  247 us
    reduce_scatter x2, waiting for transfers between devices, local(): lax.psum_scatter(ffn_term(jnp.int32(0), local_rows * lax.axis_size('tp'))...  243 us
    all_gather x2, waiting for transfers between devices, local(): normed_two_full = lax.all_gather(normed_two, 'tp', axis=0, tiled=True)  164 us
    all_gather x2, waiting for transfers between devices, local(): normed_full = lax.all_gather(normed_one, 'tp', axis=0, tiled=True)  129 us
    all_gather x2, waiting for transfers between devices, local(): grad_top_full = lax.all_gather(grad_top, 'tp', axis=0, tiled=True)  115 us
    all_gather x2, waiting for transfers between devices, local(): lax.all_gather(grad_middle.astype(jnp.bfloat16), 'tp', axis=0, tiled=True)  93.9 us
  transfers between devices with their start and end apart: 21, of which 19 were waited for; matrix products, arithmetic and copies ran while one was open for 20% of the time, Pallas kernels for 0%

commit v1 on v0

--- a/solution.py
+++ b/solution.py
@@ -3,6 +3,8 @@
 import jax
 import jax.numpy as jnp
 from jax import lax
+from jax.experimental import pallas as pl
+from jax.experimental.pallas import tpu as pltpu
 from jax.sharding import PartitionSpec as P
 
 HD = 128
@@ -352,9 +354,456 @@
     )
 
 
+QUADS = 4
+
+
+def plane_fits(mesh):
+    return mesh.shape["fsdp"] == 2 * QUADS and mesh.shape["tp"] == 4
+
+
+def flips(size, bit):
+    return [(index, index ^ bit) for index in range(size)]
+
+
+def over_quad(value, step):
+    return lax.ppermute(value, "fsdp", flips(2 * QUADS, 2 * step))
+
+
+def over_core(value):
+    return lax.ppermute(value, "fsdp", flips(2 * QUADS, 1))
+
+
+def over_pair(value):
+    return lax.ppermute(value, "tp", flips(lax.axis_size("tp"), 1))
+
+
+def ring_up(value):
+    size = lax.axis_size("tp")
+    return lax.ppermute(value, "tp", [(index, (index + 1) % size) for index in range(size)])
+
+
+def ring_down(value):
+    size = lax.axis_size("tp")
+    return lax.ppermute(value, "tp", [(index, (index - 1) % size) for index in range(size)])
+
+
+def low(value):
+    return value.astype(jnp.bfloat16)
+
+
+def wide(value):
+    return value.astype(jnp.float32)
+
+
+def mm(form, left, right):
+    return jnp.einsum(form, left, right, preferred_element_type=jnp.float32)
+
+
+def choose(first, when_true, when_false):
+    return jnp.where(first, when_true, when_false)
+
+
+def spread_rows(weight, quad):
+    rows, columns = weight.shape
+    part = columns // QUADS
+    pieces = [lax.dynamic_slice(weight, (0, quad * part), (rows, part))]
+    for step in range(1, QUADS):
+        piece = lax.dynamic_slice(weight, (0, (quad ^ step) * part), (rows, part))
+        pieces.append(over_quad(piece, step))
+    odd = (quad & 1) == 1
+    high = (quad & 2) == 2
+    ordered = []
+    for index in range(QUADS):
+        even_side = choose(odd, pieces[index ^ 1], pieces[index])
+        far_side = choose(odd, pieces[index ^ 3], pieces[index ^ 2])
+        ordered.append(choose(high, far_side, even_side))
+    return jnp.stack(ordered)
+
+
+def gather_columns(block, core):
+    pieces = [block]
+    for _ in range(lax.axis_size("tp") - 1):
+        pieces.append(ring_up(pieces[-1]))
+    whole = []
+    first = core == 0
+    quads, rows, part = block.shape
+    for piece in pieces:
+        other = over_core(piece)
+        even_rows = choose(first, piece, other)
+        odd_rows = choose(first, other, piece)
+        whole.append(jnp.stack([even_rows, odd_rows], axis=1).reshape(2 * quads * rows, part))
+    return jnp.concatenate(whole, axis=1)
+
+
+def gather_tokens(own):
+    half = own.shape[0] // 2
+    from_x = over_quad(own, 1)
+    from_y = over_quad(own, 2)
+    far_top = over_quad(from_y[:half], 1)
+    far_bottom = over_quad(from_x[half:], 2)
+    return jnp.concatenate([own, from_x, from_y, far_top, far_bottom], axis=0)
+
+
+def scatter_tokens(partial):
+    count = partial.shape[0] // QUADS
+    half = count // 2
+    here, to_x, to_y, far = [partial[index * count : (index + 1) * count] for index in range(QUADS)]
+    got_x = over_quad(low(jnp.concatenate([to_x[:half], far[:half]], axis=0)), 1)
+    got_y = over_quad(low(jnp.concatenate([to_y[half:], far[half:]], axis=0)), 2)
+    last_y = over_quad(low(wide(to_y[:half]) + wide(got_x[half:])), 2)
+    last_x = over_quad(low(wide(to_x[half:]) + wide(got_y[half:])), 1)
+    top = wide(here[:half]) + wide(got_x[:half]) + wide(last_y)
+    bottom = wide(here[half:]) + wide(got_y[:half]) + wide(last_x)
+    return jnp.concatenate([top, bottom], axis=0)
+
+
+def reduce_weight_grad(grad, core, quad):
+    size = lax.axis_size("tp")
+    rows = grad.shape[0] // (2 * QUADS)
+    part = grad.shape[1] // size
+    split = grad.reshape(QUADS, 2, rows, size * part)
+    first = core == 0
+    keep = choose(first, split[:, 0], split[:, 1])
+    send = low(choose(first, split[:, 1], split[:, 0]))
+    got = over_core(send)
+    total = keep + wide(got)
+    running = total[:, :, (size - 1) * part :]
+    for step in range(size - 2, -1, -1):
+        running = total[:, :, step * part : (step + 1) * part] + wide(ring_down(low(running)))
+    result = jnp.zeros((rows, QUADS * part), jnp.float32)
+    for step in range(QUADS):
+        piece = lax.dynamic_index_in_dim(running, quad ^ step, 0, keepdims=False)
+        if step:
+            piece = wide(over_quad(low(piece), step))
+        result = lax.dynamic_update_slice(result, piece, (0, (quad ^ step) * part))
+    return result
+
+
+def reduce_gain_grads(sums, index):
+    for bit in (4, 2, 1):
+        count = sums.shape[1] // 2
+        mine = (index & bit) // bit
+        keep = lax.dynamic_slice_in_dim(sums, mine * count, count, 1)
+        send = lax.dynamic_slice_in_dim(sums, (1 - mine) * count, count, 1)
+        sums = keep + lax.ppermute(send, "fsdp", flips(2 * QUADS, bit))
+    for bit in (1, 2):
+        sums = sums + lax.ppermute(sums, "tp", flips(lax.axis_size("tp"), bit))
+    return sums
+
+
+def turn(values, cosine, sine):
+    return values * cosine + pltpu.roll(values, values.shape[-1] // 2, 1) * sine
+
+
+def turn_back(values, cosine, sine):
+    return values * cosine - pltpu.roll(values, values.shape[-1] // 2, 1) * sine
+
+
+def dot_nt(left, right):
+    return lax.dot_general(
+        left, right, (((1,), (1,)), ((), ())), preferred_element_type=jnp.float32
+    )
+
+
+def dot_tn(left, right):
+    return lax.dot_general(
+        left, right, (((0,), (0,)), ((), ())), preferred_element_type=jnp.float32
+    )
+
+
+def allowed_of(marks_row, marks_column):
+    same = marks_column[0, :, 0:1] == marks_row[0, 0:1, :]
+    seen = marks_row[0, 1:2, :] <= marks_column[0, :, 1:2]
+    return jnp.where(same & seen, 1.0, 0.0)
+
+
+def attention_kernel(
+    shift, top, bottom, cosine, sine, marks_row, marks_column, qkv_out, mixed_out, allowed
+):
+    allowed[...] = allowed_of(marks_row, marks_column)
+    heads = top.shape[1] // (3 * HD)
+    count = top.shape[0]
+    scale = 1.0 / math.sqrt(HD)
+    for head in range(heads):
+        parts = []
+        for kind in range(3):
+            at = (3 * head + kind) * HD
+            values = jnp.concatenate([top[:, at : at + HD], bottom[:, at : at + HD]], axis=0)
+            if kind < 2:
+                values = turn(values, cosine[0], sine[0])
+            values = values.astype(jnp.bfloat16)
+            qkv_out[:, 0, :, at : at + HD] = values.reshape(2, count, HD)
+            parts.append(values)
+        query, keys, values = parts
+        scores = dot_nt(query, keys) * scale + shift
+        sigma = 1.0 / (1.0 + jnp.exp(-scores))
+        weights = (sigma * allowed[...]).astype(jnp.bfloat16)
+        mixed = jnp.dot(weights, values, preferred_element_type=jnp.float32)
+        mixed_out[:, 0, :, head * HD : (head + 1) * HD] = mixed.astype(jnp.bfloat16).reshape(
+            2, count, HD
+        )
+
+
+def attention_back_kernel(
+    shift, qkv, grad_mixed, cosine, sine, marks_row, marks_column, grad_out, allowed
+):
+    allowed[...] = allowed_of(marks_row, marks_column)
+    heads = qkv.shape[3] // (3 * HD)
+    count = qkv.shape[2]
+    scale = 1.0 / math.sqrt(HD)
+    for head in range(heads):
+        at = 3 * head * HD
+        query, keys, values = [
+            qkv[:, 0, :, at + kind * HD : at + (kind + 1) * HD].reshape(2 * count, HD)
+            for kind in range(3)
+        ]
+        grads = grad_mixed[:, 0, :, head * HD : (head + 1) * HD].reshape(2 * count, HD)
+        scores = dot_nt(query, keys) * scale + shift
+        sigma = 1.0 / (1.0 + jnp.exp(-scores))
+        kept = sigma * allowed[...]
+        weights = kept.astype(jnp.bfloat16)
+        grad_values = dot_tn(weights, grads)
+        grad_scores = (dot_nt(grads, values) * kept * (1.0 - sigma)).astype(jnp.bfloat16)
+        grad_query = jnp.dot(grad_scores, keys, preferred_element_type=jnp.float32) * scale
+        grad_keys = dot_tn(grad_scores, query) * scale
+        grad_query = turn_back(grad_query, cosine[0], sine[0])
+        grad_keys = turn_back(grad_keys, cosine[0], sine[0])
+        for kind, grad in enumerate((grad_query, grad_keys, grad_values)):
+            grad_out[:, 0, :, at + kind * HD : at + (kind + 1) * HD] = grad.astype(
+                jnp.bfloat16
+            ).reshape(2, count, HD)
+
+
+def token_block(count, columns):
+    return pl.BlockSpec((2, 1, count, columns), lambda quad: (0, quad, 0, 0))
+
+
+def piece_block(shape):
+    return pl.BlockSpec((1,) + shape[1:], lambda quad: (quad, 0, 0))
+
+
+def attention(top, bottom, cosine, sine, marks_row, marks_column, shift):
+    count = top.shape[0] // QUADS
+    columns = top.shape[1]
+    width = columns // 3
+    pairs = QUADS * (2 * count) * (2 * count) * (width // HD)
+    return pl.pallas_call(
+        lambda *refs: attention_kernel(shift, *refs),
+        grid=(QUADS,),
+        in_specs=[
+            pl.BlockSpec((count, columns), lambda quad: (quad, 0)),
+            pl.BlockSpec((count, columns), lambda quad: (quad, 0)),
+            piece_block(cosine.shape),
+            piece_block(sine.shape),
+            piece_block(marks_row.shape),
+            piece_block(marks_column.shape),
+        ],
+        out_specs=[token_block(count, columns), token_block(count, width)],
+        out_shape=[
+            jax.ShapeDtypeStruct((2, QUADS, count, columns), jnp.bfloat16),
+            jax.ShapeDtypeStruct((2, QUADS, count, width), jnp.bfloat16),
+        ],
+        scratch_shapes=[pltpu.VMEM((2 * count, 2 * count), jnp.float32)],
+        cost_estimate=pl.CostEstimate(
+            flops=4 * HD * pairs, bytes_accessed=24 * QUADS * count * columns, transcendentals=pairs
+        ),
+        name="attention",
+    )(top, bottom, cosine, sine, marks_row, marks_column)
+
+
+def attention_back(qkv, grad_mixed, cosine, sine, marks_row, marks_column, shift):
+    _, _, count, columns = qkv.shape
+    width = columns // 3
+    pairs = QUADS * (2 * count) * (2 * count) * (width // HD)
+    return pl.pallas_call(
+        lambda *refs: attention_back_kernel(shift, *refs),
+        grid=(QUADS,),
+        in_specs=[
+            token_block(count, columns),
+            token_block(count, width),
+            piece_block(cosine.shape),
+            piece_block(sine.shape),
+            piece_block(marks_row.shape),
+            piece_block(marks_column.shape),
+        ],
+        out_specs=token_block(count, columns),
+        out_shape=jax.ShapeDtypeStruct(qkv.shape, jnp.bfloat16),
+        scratch_shapes=[pltpu.VMEM((2 * count, 2 * count), jnp.float32)],
+        cost_estimate=pl.CostEstimate(
+            flops=10 * HD * pairs, bytes_accessed=12 * QUADS * count * columns, transcendentals=pairs
+        ),
+        name="attention_back",
+    )(qkv, grad_mixed, cosine, sine, marks_row, marks_column)
+
+
+def plane(
+    inputs,
+    cotangent,
+    segment_ids,
+    block_ids,
+    positions,
+    w_qkv,
+    w_out,
+    w_gateup,
+    w_down,
+    gain_attn,
+    gain_ffn,
+):
+    _, _, rows, width = inputs.shape
+    length = segment_ids.shape[2]
+    shard = w_qkv.shape[0]
+    place = lax.axis_index("fsdp")
+    column = lax.axis_index("tp")
+    core = place % 2
+    quad = place // 2
+    first = (column % 2) == 0
+    shift = -math.log(length)
+
+    def own_first(pair):
+        return choose(first, pair[0], pair[1]), choose(first, pair[1], pair[0])
+
+    def half_marks(marks):
+        line = choose(first, marks[0, 0], marks[1, 0])
+        own = lax.dynamic_slice_in_dim(line, column * rows, rows, 0)
+        other = lax.dynamic_slice_in_dim(line, (column ^ 1) * rows, rows, 0)
+        return [wide(own), wide(other)]
+
+    small = jnp.concatenate(
+        [wide(gain_attn), wide(gain_ffn)]
+        + half_marks(segment_ids)
+        + half_marks(block_ids)
+        + half_marks(positions)
+    )
+    table = lax.all_gather(small, "fsdp")
+    gain_one = table[:, :shard].reshape(width)
+    gain_two = table[:, shard : 2 * shard].reshape(width)
+    marks = jnp.stack(
+        [
+            lax.dynamic_index_in_dim(table, place ^ (2 * step), 0, keepdims=False)[2 * shard :]
+            for step in range(QUADS)
+        ]
+    ).reshape(QUADS, 3, 2 * rows)
+    marks_row = marks[:, :2]
+    marks_column = marks_row.transpose(0, 2, 1)
+    ladder = jnp.arange(HD // 2, dtype=jnp.float32) * (2.0 / HD)
+    angles = marks[:, 2, :, None] * jnp.exp(-math.log(rope_base) * ladder)
+    cosine = jnp.cos(angles)
+    sine = jnp.sin(angles)
+    cosine = jnp.concatenate([cosine, cosine], axis=-1)
+    sine = jnp.concatenate([-sine, sine], axis=-1)
+
+    part_qkv = spread_rows(
+        w_qkv.reshape(shard, 3, QUADS, -1).transpose(0, 2, 1, 3).reshape(shard, -1), quad
+    )
+    full_qkv = gather_columns(part_qkv, core)
+    full_out = gather_columns(spread_rows(w_out, quad), core)
+    full_gate = gather_columns(spread_rows(w_gateup[:, 0], quad), core)
+    full_up = gather_columns(spread_rows(w_gateup[:, 1], quad), core)
+    full_down = gather_columns(spread_rows(w_down, quad), core)
+
+    residual = [wide(value) for value in own_first(inputs[:, 0])]
+    norm_one = [normalize(value) for value in residual]
+    normed_one = [low(unit * gain_one) for unit, _ in norm_one]
+    top_one = gather_tokens(normed_one[0])
+    bottom_one = gather_tokens(over_pair(normed_one[1]))
+    qkv, mixed = attention(
+        mm("td,de->te", top_one, full_qkv),
+        mm("td,de->te", bottom_one, full_qkv),
+        cosine,
+        sine,
+        marks_row,
+        marks_column,
+        shift,
+    )
+    count = QUADS * rows
+    mixed_all = mixed.reshape(2 * count, -1)
+    term = low(mm("tc,dc->td", mixed_all, full_out))
+    other_half = over_pair(low(scatter_tokens(term[count:])))
+    own_half = scatter_tokens(term[:count])
+    middle = [residual[0] + own_half, residual[1] + wide(other_half)]
+
+    norm_two = [normalize(value) for value in middle]
+    normed_two = [low(unit * gain_two) for unit, _ in norm_two]
+    grad_top = own_first(cotangent[:, 0])
+    results = [None, None]
+    grad_middle = [None, None]
+    ffn = [None, None]
+    gain_two_sum = 0.0
+    for side in (1, 0):
+        tokens = gather_tokens(normed_two[side])
+        tops = gather_tokens(grad_top[side])
+        gate = mm("td,df->tf", tokens, full_gate)
+        up = mm("td,df->tf", tokens, full_up)
+        sigma = jax.nn.sigmoid(gate)
+        silu = gate * sigma
+        hidden = low(silu * up)
+        grad_hidden = mm("td,df->tf", tops, full_down)
+        grad_gate = low(grad_hidden * up * sigma * (1.0 + gate * (1.0 - sigma)))
+        grad_up = low(grad_hidden * silu)
+        back = low(mm("tf,df->td", grad_gate, full_gate) + mm("tf,df->td", grad_up, full_up))
+        grad_normed = scatter_tokens(back)
+        unit, factor = norm_two[side]
+        grad_middle[side] = wide(grad_top[side]) + normalize_back(grad_normed, unit, factor, gain_two)
+        gain_two_sum = gain_two_sum + jnp.sum(grad_normed * unit, axis=0)
+        results[side] = low(
+            middle[side] + scatter_tokens(low(mm("tf,df->td", hidden, full_down)))
+        )
+        ffn[side] = (tokens, tops, hidden, grad_gate, grad_up)
+    tokens_two, tops_all, hidden_all, grad_gate_all, grad_up_all = [
+        jnp.concatenate(both, axis=0) for both in zip(*ffn)
+    ]
+    grad_down = reduce_weight_grad(mm("td,tf->df", tops_all, hidden_all), core, quad)
+    grad_gate_rows = reduce_weight_grad(mm("td,tf->df", tokens_two, grad_gate_all), core, quad)
+    grad_up_rows = reduce_weight_grad(mm("td,tf->df", tokens_two, grad_up_all), core, quad)
+
+    grad_low = [low(value) for value in grad_middle]
+    grad_all = jnp.concatenate(
+        [gather_tokens(grad_low[0]), gather_tokens(over_pair(grad_low[1]))], axis=0
+    )
+    grad_mixed = low(mm("td,dc->tc", grad_all, full_out))
+    grad_qkv = attention_back(
+        qkv,
+        grad_mixed.reshape(mixed.shape),
+        cosine,
+        sine,
+        marks_row,
+        marks_column,
+        shift,
+    ).reshape(2 * count, -1)
+    term = low(mm("te,de->td", grad_qkv, full_qkv))
+    other_half = over_pair(low(scatter_tokens(term[count:])))
+    grad_normed_one = [scatter_tokens(term[:count]), wide(other_half)]
+    grad_inputs = [
+        grad_middle[side]
+        + normalize_back(grad_normed_one[side], norm_one[side][0], norm_one[side][1], gain_one)
+        for side in range(2)
+    ]
+    gain_one_sum = jnp.sum(grad_normed_one[0] * norm_one[0][0], axis=0) + jnp.sum(
+        grad_normed_one[1] * norm_one[1][0], axis=0
+    )
+    grad_out_rows = reduce_weight_grad(mm("td,tc->dc", grad_all, mixed_all), core, quad)
+    tokens_one = jnp.concatenate([top_one, bottom_one], axis=0)
+    grad_qkv_rows = reduce_weight_grad(mm("td,te->de", tokens_one, grad_qkv), core, quad)
+    grad_qkv_rows = (
+        grad_qkv_rows.reshape(shard, QUADS, 3, -1).transpose(0, 2, 1, 3).reshape(w_qkv.shape)
+    )
+    gains = reduce_gain_grads(jnp.stack([gain_one_sum, gain_two_sum]), place)
+    return (
+        jnp.stack(own_first(results))[:, None],
+        jnp.stack(own_first(grad_inputs))[:, None],
+        grad_qkv_rows,
+        grad_out_rows,
+        jnp.stack([grad_gate_rows, grad_up_rows], axis=1),
+        grad_down,
+        gains[0],
+        gains[1],
+    )
+
+
 def solution(mesh):
+    body = plane if plane_fits(mesh) else local
     return jax.shard_map(
-        local,
+        body,
         mesh=mesh,
         in_specs=(
             P(None, "fsdp", "tp", None),

time: 2640 us -> 1450 us (0.55)
  waiting for transfers between devices: 1870 us -> 551 us
  starting transfers between devices: 0.86 us -> 149 us
  matrix products: 398 us -> 325 us
  local copies, waits for them, and re-layouts: 125 us -> 185 us
  blocking collectives: 65.3 us -> 24.9 us
  Pallas kernels: 0 us -> 32.8 us
  other arithmetic: 146 us -> 176 us
    reduce_scatter x9 -> x0, waiting for transfers between devices: 1180 us -> none  [the longest x1 376 us: local(): lax.psum_scatter(grad_rows([record], shard_rows * lax.axis_size('fsdp')),...]
    all_gather x12 -> x0, waiting for transfers between devices: 688 us -> none  [the longest x2 164 us: local(): normed_two_full = lax.all_gather(normed_two, 'tp', axis=0, tiled=True)]
    ppermute x0 -> x158, waiting for transfers between devices: none -> 551 us  [the longest x94 303 us: over_quad(): return lax.ppermute(value, 'fsdp', flips(2 * QUADS, 2 * step))]
    ppermute x0 -> x158, starting transfers between devices: none -> 149 us  [the longest x94 111 us: over_quad(): return lax.ppermute(value, 'fsdp', flips(2 * QUADS, 2 * step))]
    dot_general x48 -> x22, matrix products: 398 us -> 325 us  [mm(): return jnp.einsum(form, left, right, preferred_element_type=jnp.float32)]
    psum x1 -> x0, blocking collectives: 45.9 us -> none  [local(): gain_totals = lax.psum((gain_one_total, gain_two_total), ('fsdp', 'tp'))]
    pallas_call x0 -> x2, Pallas kernels: none -> 32.8 us  [the longest x1 20 us: attention_back(): pl.pallas_call(lambda *refs: attention_back_kernel(shift, *refs), grid=(Q...]
    convert_element_type x6 -> x26, other arithmetic: 8.9 us -> 39.6 us  [the longest x23 39.6 us: low(): return value.astype(jnp.bfloat16)]
  transfers between devices with their start and end apart: 21 -> 158, of which waited for: 19 -> 68; matrix products, arithmetic and copies ran while one was open for 20% -> 46% of each run, Pallas kernels for 0% -> 2%
where the time goes in v1:
time: 1450 us
  waiting for transfers between devices  551 us (38%)
  matrix products  325 us (22%)
  local copies, waits for them, and re-layouts  185 us (13%)
  other arithmetic  176 us (12%)
  starting transfers between devices  149 us (10%)
  Pallas kernels  32.8 us (2%)
  blocking collectives  24.9 us (2%)
    dot_general x22, matrix products, mm(): return jnp.einsum(form, left, right, preferred_element_type=jnp.float32)  325 us
    ppermute x94, waiting for transfers between devices, over_quad(): return lax.ppermute(value, 'fsdp', flips(2 * QUADS, 2 * step))  303 us
    ppermute x15, waiting for transfers between devices, ring_down(): lax.ppermute(value, 'tp', [(index, (index - 1) % size) for index in range...  138 us
    ppermute x94, starting transfers between devices, over_quad(): return lax.ppermute(value, 'fsdp', flips(2 * QUADS, 2 * step))  111 us
    ppermute x15, waiting for transfers between devices, ring_up(): lax.ppermute(value, 'tp', [(index, (index + 1) % size) for index in range...  100 us
    unnamed x346, local copies, waits for them, and re-layouts  73.7 us
    convert_element_type x23, other arithmetic, low(): return value.astype(jnp.bfloat16)  39.6 us
    add x5, other arithmetic, reduce_weight_grad(): total = keep + wide(got)  29.9 us
  transfers between devices with their start and end apart: 158, of which 68 were waited for; matrix products, arithmetic and copies ran while one was open for 46% of the time, Pallas kernels for 2%

profile of v1, /device:TPU:0, one launch (start us, length us, event | category | flops | bytes accessed | tf_op | source)
XLA Modules:
  0.0 1447.6 jit_solution(16015796441178010211)
XLA Ops:
  13.8 24.9 %all-gather = f32[16384]{0:T(1024)S(1)} all-gather(f32[2048]{0:T(1024)S(1)} %constant_dynamic-update-slice_fusion.78), channel_id=2, replica_groups=mesh['fsdp'=8,'tp'=4] {'fsdp'}, dimensions={0}, use_global_device_ids=true | all-gather | bytes 73728 | tf_op jit(solution)/shard_map/all_gather | solution.py:677
  61.2 7.0 fusion.110
  137.9 7.6 collective-permute-done.25
  164.3 8.6 collective-permute-done.1
  174.0 8.0 collective-permute-done.27
  196.2 8.2 collective-permute-done.86
  212.5 9.2 collective-permute-done.2
  228.7 15.2 %collective-permute-done.41 = bf16[4,256,512]{2,1,0:T(8,128)(2,1)} collective-permute-done((bf16[4,256,512]{2,1,0:T(8,128)(2,1)S(1)}, bf16[4,256,512]{2,1,0:T(8,128)(2,1)}, u32[]{:S(2)}, u32[]{:S(2)}) %collective-permute-start.41) | collective-permute-done | bytes 1048608 | tf_op jit(solution)/shard_map/ppermute | solution.py:382
  245.0 20.3 %collective-permute-done.61 = bf16[4,256,512]{2,1,0:T(8,128)(2,1)} collective-permute-done((bf16[4,256,512]{2,1,0:T(8,128)(2,1)S(1)}, bf16[4,256,512]{2,1,0:T(8,128)(2,1)}, u32[]{:S(2)}, u32[]{:S(2)}) %collective-permute-start.61) | collective-permute-done | bytes 1048608 | tf_op jit(solution)/shard_map/ppermute | solution.py:382
  300.0 9.1 collective-permute-done.97
  326.2 12.3 copy.291
  342.5 12.8 collective-permute-done.43
  360.0 11.8 fusion.90.refs_1_
  371.9 9.2 fusion.91.refs_0_
  381.0 12.7 attention.1
  407.4 15.3 %collective-permute-done.45 = bf16[4,256,512]{2,1,0:T(8,128)(2,1)} collective-permute-done((bf16[4,256,512]{2,1,0:T(8,128)(2,1)}, bf16[4,256,512]{2,1,0:T(8,128)(2,1)}, u32[]{:S(2)}, u32[]{:S(2)}) %collective-permute-start.45) | collective-permute-done | bytes 1048608 | tf_op jit(solution)/shard_map/ppermute | solution.py:382
  431.5 13.2 collective-permute-done.65
  449.5 21.7 %collective-permute-done.73 = bf16[256,2048]{1,0:T(8,128)(2,1)S(1)} collective-permute-done((bf16[256,2048]{1,0:T(8,128)(2,1)S(1)}, bf16[256,2048]{1,0:T(8,128)(2,1)S(1)}, u32[]{:S(2)}, u32[]{:S(2)}) %collective-permute-start.73) | collective-permute-done | bytes 1048608 | tf_op jit(solution)/shard_map/ppermute | solution.py:369
  471.3 9.5 collective-permute-done.72
  498.0 8.3 collective-permute-done.74
  515.5 15.1 %collective-permute-done.34 = bf16[256,2048]{1,0:T(8,128)(2,1)S(1)} collective-permute-done((bf16[256,2048]{1,0:T(8,128)(2,1)S(1)}, bf16[256,2048]{1,0:T(8,128)(2,1)S(1)}, u32[]{:S(2)}, u32[]{:S(2)}) %collective-permute-start.34) | collective-permute-done | bytes 1048608 | tf_op jit(solution)/shard_map/ppermute | solution.py:369
  534.2 7.4 collective-permute-done.35
  547.6 14.1 fusion.95
  561.8 13.9 fusion.99
  575.7 19.5 %multiply_convert_fusion.2 = (bf16[1024,2048]{1,0:T(8,128)(2,1)}, bf16[1024,2048]{1,0:T(8,128)(2,1)}, bf16[1024,2048]{1,0:T(8,128)(2,1)}) fusion(f32[1024,2048]{1,0:T(8,128)} %fusion.99, f32[1024,2048]{1,0:T(8,128)} %fusion.95, bf16[1024,2048]{1,0:T(8,128)(2,1)} %get-tuple-element.282, bf16[2048,512]{1,0:T(8,128)(2,1)} %bitcast.516, ...), kind=kOutput, calls=%fused_computation.31 | convolution fusion | flops 8654946304 | bytes 41943040 | tf_op jit(solution)/shard_map/td,df->tf/dot_general | solution.py:399
  595.2 14.0 fusion.97
  609.3 13.8 add_convert_fusion.1
  626.2 12.2 convolution_convert_fusion.3
  653.6 19.3 %collective-permute-done.67 = bf16[256,2048]{1,0:T(8,128)(2,1)S(1)} collective-permute-done((bf16[256,2048]{1,0:T(8,128)(2,1)S(1)}, bf16[256,2048]{1,0:T(8,128)(2,1)S(1)}, u32[]{:S(2)}, u32[]{:S(2)}) %collective-permute-start.67) | collective-permute-done | bytes 1048608 | tf_op jit(solution)/shard_map/ppermute | solution.py:369
  681.7 19.0 %collective-permute-done.79 = bf16[128,2048]{1,0:T(8,128)(2,1)S(1)} collective-permute-done((bf16[128,2048]{1,0:T(8,128)(2,1)S(1)}, bf16[128,2048]{1,0:T(8,128)(2,1)S(1)}, u32[]{:S(2)}, u32[]{:S(2)}) %collective-permute-start.79) | collective-permute-done | bytes 524320 | tf_op jit(solution)/shard_map/ppermute | solution.py:369
  703.6 14.0 fusion.94
  717.6 13.9 fusion.98
  731.5 19.5 %multiply_convert_fusion = (bf16[1024,2048]{1,0:T(8,128)(2,1)}, bf16[1024,2048]{1,0:T(8,128)(2,1)}, bf16[1024,2048]{1,0:T(8,128)(2,1)}) fusion(f32[1024,2048]{1,0:T(8,128)} %fusion.98, f32[1024,2048]{1,0:T(8,128)} %fusion.94, bf16[1024,2048]{1,0:T(8,128)(2,1)} %get-tuple-element.264, bf16[2048,512]{1,0:T(8,128)(2,1)} %bitcast.518, ...), kind=kOutput, calls=%fused_computation.28 | convolution fusion | flops 8654946304 | bytes 41943040 | tf_op jit(solution)/shard_map/td,df->tf/dot_general | solution.py:399
  751.0 14.0 fusion.96
  765.0 24.5 %fusion = f32[2048,2048]{1,0:T(8,128)} fusion(bf16[2048,2048]{1,0:T(8,128)(2,1)} %get-tuple-element.267, bf16[1024,2048]{1,0:T(8,128)(2,1)} %get-tuple-element.100, bf16[1024,2048]{1,0:T(8,128)(2,1)} %get-tuple-element.97), kind=kOutput, calls=%fused_computation.9 | convolution fusion | flops 17196646400 | bytes 33554432 | tf_op jit(solution)/shard_map/td,tf->df/dot_general | solution.py:399
  789.5 20.6 %fusion.4 = f32[2048,2048]{1,0:T(8,128)} fusion(bf16[2048,2048]{1,0:T(8,128)(2,1)S(1)} %bitcast.561, bf16[1024,2048]{1,0:T(8,128)(2,1)S(1)} %copy-done.135, bf16[1024,2048]{1,0:T(8,128)(2,1)S(1)} %copy-done.134), kind=kOutput, calls=%fused_computation.13 | convolution fusion | flops 17196646400 | bytes 33554432 | tf_op jit(solution)/shard_map/td,tf->df/dot_general | solution.py:399
  810.1 14.2 add_convert_fusion
  837.3 11.6 convolution_convert_fusion.2
  850.4 23.6 %fusion.8 = f32[2048,2048]{1,0:T(8,128)S(1)} fusion(bf16[2048,2048]{1,0:T(8,128)(2,1)} %get-tuple-element.263, bf16[1024,2048]{1,0:T(8,128)(2,1)} %get-tuple-element.101, bf16[1024,2048]{1,0:T(8,128)(2,1)} %get-tuple-element.98), kind=kOutput, calls=%fused_computation.17 | convolution fusion | flops 17196646400 | bytes 33554432 | tf_op jit(solution)/shard_map/td,tf->df/dot_general | solution.py:399
  900.4 7.7 collective-permute-done.81
  914.4 8.5 collective-permute-done.83
  934.0 8.4 fusion.16
  945.1 8.5 collective-permute-done.93
  960.4 7.6 collective-permute-done.94
  971.7 22.1 %collective-permute-done.106 = bf16[256,2048]{1,0:T(8,128)(2,1)S(1)} collective-permute-done((bf16[256,2048]{1,0:T(8,128)(2,1)}, bf16[256,2048]{1,0:T(8,128)(2,1)S(1)}, u32[]{:S(2)}, u32[]{:S(2)}) %collective-permute-start.106) | collective-permute-done | bytes 1048608 | tf_op jit(solution)/shard_map/ppermute | solution.py:369
  1001.0 8.6 bitcast_add_fusion
  1013.2 8.6 bitcast_add_fusion.2
  1035.9 9.4 convolution_convert_fusion.4
  1045.3 20.0 %attention_back.1 = bf16[2,4,256,1536]{3,2,1,0:T(8,128)(2,1)} custom-call(bf16[2,4,256,1536]{3,2,1,0:T(8,128)(2,1)} %get-tuple-element.11.refs_0_, bf16[2,4,256,512]{3,2,1,0:T(8,128)(2,1)} %bitcast.578, f32[4,512,128]{2,1,0:T(8,128)} %pad_maximum_fusion.26.refs_2_, f32[4,512,128]{2,1,0:T(8,128)} %pad_maximum_fusion.27.refs_3_, f32[4,2,512]{2,1,0:T(2,128)} %copy.237.refs_4_, ...), custom_call_target="tpu_custom_call" | custom-call | flops 5368709120 | bytes 18874368 | tf_op jit(solution)/shard_map/attention_back/pallas_call | solution.py:618
  1065.4 17.7 %convolution_convert_fusion = bf16[2048,2048]{1,0:T(8,128)(2,1)S(1)} fusion(bf16[2048,1536]{1,0:T(8,128)(2,1)} %bitcast.576, bf16[2048,384]{1,0:T(8,128)(2,1)} %bitcast.538, bf16[2048,384]{1,0:T(8,128)(2,1)} %bitcast.535, bf16[2048,384]{1,0:T(8,128)(2,1)} %bitcast.532, bf16[2048,384]{1,0:T(8,128)(2,1)} %bitcast.528), kind=kOutput, calls=%fused_computation.39 | convolution fusion | flops 12914262016 | bytes 20971520 | tf_op jit(solution)/shard_map/te,de->td/dot_general | solution.py:399
  1091.1 12.3 copy.292
  1103.3 7.5 fusion.113
  1110.9 19.1 %fusion.112 = f32[4,2,256,1536]{3,2,1,0:T(8,128)} fusion(bf16[4,2,256,2048]{3,2,1,0:T(8,128)(2,1)} %bitcast.473, bf16[2048,1536,1,1]{1,0,3,2:T(8,128)(2,1)} %bitcast.577), kind=kOutput, calls=%fused_computation.539 | convolution fusion | flops 12884901888 | bytes 27262976 | tf_op jit(solution)/shard_map/td,te->de/dot_general | solution.py:399
  1130.1 7.0 fusion.19
  1157.6 7.3 collective-permute-done.113
  1168.6 9.9 collective-permute-done.110
  1181.6 48.2 %collective-permute-done.127 = bf16[4,256,128]{2,1,0:T(8,128)(2,1)S(1)} collective-permute-done((bf16[4,256,128]{2,1,0:T(8,128)(2,1)S(1)}, bf16[4,256,128]{2,1,0:T(8,128)(2,1)S(1)}, u32[]{:S(2)}, u32[]{:S(2)}) %collective-permute-start.127) | collective-permute-done | bytes 262176 | tf_op jit(solution)/shard_map/ppermute | solution.py:387
  1242.9 11.4 collective-permute-done.129
  1273.6 18.0 %collective-permute-done.149 = bf16[4,256,512]{2,1,0:T(8,128)(2,1)S(1)} collective-permute-done((bf16[4,256,512]{2,1,0:T(8,128)(2,1)S(1)}, bf16[4,256,512]{2,1,0:T(8,128)(2,1)S(1)}, u32[]{:S(2)}, u32[]{:S(2)}) %collective-permute-start.149) | collective-permute-done | bytes 1048608 | tf_op jit(solution)/shard_map/ppermute | solution.py:387
  1293.7 20.4 %collective-permute-done.135 = bf16[4,256,512]{2,1,0:T(8,128)(2,1)S(1)} collective-permute-done((bf16[4,256,512]{2,1,0:T(8,128)(2,1)S(1)}, bf16[4,256,512]{2,1,0:T(8,128)(2,1)S(1)}, u32[]{:S(2)}, u32[]{:S(2)}) %collective-permute-start.135) | collective-permute-done | bytes 1048608 | tf_op jit(solution)/shard_map/ppermute | solution.py:387
  1316.2 20.4 %collective-permute-done.142 = bf16[4,256,512]{2,1,0:T(8,128)(2,1)S(1)} collective-permute-done((bf16[4,256,512]{2,1,0:T(8,128)(2,1)S(1)}, bf16[4,256,512]{2,1,0:T(8,128)(2,1)S(1)}, u32[]{:S(2)}, u32[]{:S(2)}) %collective-permute-start.142) | collective-permute-done | bytes 1048608 | tf_op jit(solution)/shard_map/ppermute | solution.py:387
  1346.2 7.1 collective-permute-start.143
  1377.9 7.4 fusion.15
  1404.9 15.6 %collective-permute-done.120 = bf16[4,256,384]{2,1,0:T(8,128)(2,1)S(1)} collective-permute-done((bf16[4,256,384]{2,1,0:T(8,128)(2,1)S(1)}, bf16[4,256,384]{2,1,0:T(8,128)(2,1)S(1)}, u32[]{:S(2)}, u32[]{:S(2)}) %collective-permute-start.120) | collective-permute-done | bytes 786464 | tf_op jit(solution)/shard_map/ppermute | solution.py:387
  (908 shorter events, 555.6 us)
Async XLA Ops:
  3.9 150.5 %collective-permute-start.84 = (bf16[256,2048]{1,0:T(8,128)(2,1)S(1)}, bf16[256,2048]{1,0:T(8,128)(2,1)}, u32[]{:S(2)}, u32[]{:S(2)}) collective-permute-start(bf16[256,2048]{1,0:T(8,128)(2,1)S(1)} %get-tuple-element.67), channel_id=1, source_target_pairs={{0,8},{4,12},{8,0},{12,4},{16,24},{20,28},{24,16},{28,20},{1,9},{5... | collective-permute-start | bytes 3145736 | tf_op jit(solution)/shard_map/ppermute | solution.py:369
  6.8 150.5 %collective-permute-start.85 = (bf16[256,2048]{1,0:T(8,128)(2,1)S(1)}, bf16[256,2048]{1,0:T(8,128)(2,1)}, u32[]{:S(2)}, u32[]{:S(2)}) collective-permute-start(bf16[256,2048]{1,0:T(8,128)(2,1)S(1)} %get-tuple-element.67), channel_id=1, source_target_pairs={{0,16},{4,20},{8,24},{12,28},{16,0},{20,4},{24,8},{28,12},{1,17},{... | collective-permute-start | bytes 3145736 | tf_op jit(solution)/shard_map/ppermute | solution.py:369
  9.0 77.2 %collective-permute-start.19 = (bf16[256,128]{1,0:T(8,128)(2,1)}, bf16[256,128]{1,0:T(8,128)(2,1)S(1)}, u32[]{:S(2)}, u32[]{:S(2)}) collective-permute-start(bf16[256,128]{1,0:T(8,128)(2,1)} %get-tuple-element.308), channel_id=1, source_target_pairs={{0,24},{4,28},{8,16},{12,20},{16,8},{20,12},{24,0},{28,4},{1,25},{... | collective-permute-start | bytes 196616 | tf_op jit(solution)/shard_map/ppermute | solution.py:369
  9.1 78.8 %collective-permute-start.20 = (bf16[256,128]{1,0:T(8,128)(2,1)}, bf16[256,128]{1,0:T(8,128)(2,1)S(1)}, u32[]{:S(2)}, u32[]{:S(2)}) collective-permute-start(bf16[256,128]{1,0:T(8,128)(2,1)} %get-tuple-element.307), channel_id=1, source_target_pairs={{0,16},{4,20},{8,24},{12,28},{16,0},{20,4},{24,8},{28,12},{1,17},{... | collective-permute-start | bytes 196616 | tf_op jit(solution)/shard_map/ppermute | solution.py:369
  11.0 77.2 %collective-permute-start.21 = (bf16[256,128]{1,0:T(8,128)(2,1)}, bf16[256,128]{1,0:T(8,128)(2,1)}, u32[]{:S(2)}, u32[]{:S(2)}) collective-permute-start(bf16[256,128]{1,0:T(8,128)(2,1)} %get-tuple-element.306), channel_id=1, source_target_pairs={{0,8},{4,12},{8,0},{12,4},{16,24},{20,28},{24,16},{28,20},{1,9},{5... | collective-permute-start | bytes 196616 | tf_op jit(solution)/shard_map/ppermute | solution.py:369
  145.5 36.6 %collective-permute-start = (bf16[256,2048]{1,0:T(8,128)(2,1)S(1)}, bf16[256,2048]{1,0:T(8,128)(2,1)S(1)}, u32[]{:S(2)}, u32[]{:S(2)}) collective-permute-start(bf16[256,2048]{1,0:T(8,128)(2,1)S(1)} %copy-done.33), channel_id=1, source_target_pairs={{0,8},{4,12},{8,0},{12,4},{16,24},{20,28},{24,16},{28,20},{1,9},{5... | collective-permute-start | bytes 3145736 | tf_op jit(solution)/shard_map/ppermute | solution.py:369
  150.1 59.5 %collective-permute-start.14 = (bf16[256,2048]{1,0:T(8,128)(2,1)}, bf16[256,2048]{1,0:T(8,128)(2,1)}, u32[]{:S(2)}, u32[]{:S(2)}) collective-permute-start(bf16[256,2048]{1,0:T(8,128)(2,1)} %fusion.38), channel_id=1, source_target_pairs={{0,1},{1,0},{2,3},{3,2},{4,5},{5,4},{6,7},{7,6},{8,9},{9,8},{10,11... | collective-permute-start | bytes 3145736 | tf_op jit(solution)/shard_map/ppermute | solution.py:377
  172.9 36.1 %collective-permute-start.8 = (bf16[4,256,384]{1,2,0:T(8,128)(2,1)S(1)}, bf16[4,256,384]{1,2,0:T(8,128)(2,1)}, u32[]{:S(2)}, u32[]{:S(2)}) collective-permute-start(bf16[4,256,384]{1,2,0:T(8,128)(2,1)S(1)} %copy-done.98), channel_id=1, source_target_pairs={{0,1},{1,2},{2,3},{3,0},{4,5},{5,6},{6,7},{7,4},{8,9},{9,10},{10,1... | collective-permute-start | bytes 2359304 | tf_op jit(solution)/shard_map/ppermute | solution.py:382
  204.4 39.5 %collective-permute-start.41 = (bf16[4,256,512]{2,1,0:T(8,128)(2,1)S(1)}, bf16[4,256,512]{2,1,0:T(8,128)(2,1)}, u32[]{:S(2)}, u32[]{:S(2)}) collective-permute-start(bf16[4,256,512]{2,1,0:T(8,128)(2,1)S(1)} %copy-done.94), channel_id=1, source_target_pairs={{0,1},{1,2},{2,3},{3,0},{4,5},{5,6},{6,7},{7,4},{8,9},{9,10},{10,1... | collective-permute-start | bytes 3145736 | tf_op jit(solution)/shard_map/ppermute | solution.py:382
  205.6 59.8 %collective-permute-start.61 = (bf16[4,256,512]{2,1,0:T(8,128)(2,1)S(1)}, bf16[4,256,512]{2,1,0:T(8,128)(2,1)}, u32[]{:S(2)}, u32[]{:S(2)}) collective-permute-start(bf16[4,256,512]{2,1,0:T(8,128)(2,1)S(1)} %copy-done.93), channel_id=1, source_target_pairs={{0,1},{1,2},{2,3},{3,0},{4,5},{5,6},{6,7},{7,4},{8,9},{9,10},{10,1... | collective-permute-start | bytes 3145736 | tf_op jit(solution)/shard_map/ppermute | solution.py:382
  221.8 43.7 %collective-permute-start.9 = (bf16[4,256,384]{1,2,0:T(8,128)(2,1)}, bf16[4,256,384]{1,2,0:T(8,128)(2,1)S(1)}, u32[]{:S(2)}, u32[]{:S(2)}) collective-permute-start(bf16[4,256,384]{1,2,0:T(8,128)(2,1)} %collective-permute-done.8), channel_id=1, source_target_pairs={{0,4},{4,0},{8,12},{12,8},{16,20},{20,16},{24,28},{28,24},{1,5},{5... | collective-permute-start | bytes 2359304 | tf_op jit(solution)/shard_map/ppermute | solution.py:373
  222.8 48.1 %collective-permute-start.15 = (bf16[256,2048]{1,0:T(8,128)(2,1)}, bf16[256,2048]{1,0:T(8,128)(2,1)}, u32[]{:S(2)}, u32[]{:S(2)}) collective-permute-start(bf16[256,2048]{1,0:T(8,128)(2,1)} %collective-permute-done.14), channel_id=1, source_target_pairs={{0,8},{4,12},{8,0},{12,4},{16,24},{20,28},{24,16},{28,20},{1,9},{5... | collective-permute-start | bytes 3145736 | tf_op jit(solution)/shard_map/ppermute | solution.py:369
  223.4 45.2 %collective-permute-start.16 = (bf16[256,2048]{1,0:T(8,128)(2,1)}, bf16[256,2048]{1,0:T(8,128)(2,1)}, u32[]{:S(2)}, u32[]{:S(2)}) collective-permute-start(bf16[256,2048]{1,0:T(8,128)(2,1)} %collective-permute-done.14), channel_id=1, source_target_pairs={{0,16},{4,20},{8,24},{12,28},{16,0},{20,4},{24,8},{28,12},{1,17},{... | collective-permute-start | bytes 3145736 | tf_op jit(solution)/shard_map/ppermute | solution.py:369
  244.0 42.4 %collective-permute-start.52 = (bf16[4,256,512]{2,1,0:T(8,128)(2,1)}, bf16[4,256,512]{2,1,0:T(8,128)(2,1)}, u32[]{:S(2)}, u32[]{:S(2)}) collective-permute-start(bf16[4,256,512]{2,1,0:T(8,128)(2,1)} %collective-permute-done.51), channel_id=1, source_target_pairs={{0,4},{4,0},{8,12},{12,8},{16,20},{20,16},{24,28},{28,24},{1,5},{5... | collective-permute-start | bytes 3145736 | tf_op jit(solution)/shard_map/ppermute | solution.py:373
  270.9 41.0 %collective-permute-start.96 = (bf16[256,2048]{1,0:T(8,128)(2,1)S(1)}, bf16[256,2048]{1,0:T(8,128)(2,1)}, u32[]{:S(2)}, u32[]{:S(2)}) collective-permute-start(bf16[256,2048]{1,0:T(8,128)(2,1)S(1)} %get-tuple-element.65), channel_id=1, source_target_pairs={{0,8},{4,12},{8,0},{12,4},{16,24},{20,28},{24,16},{28,20},{1,9},{5... | collective-permute-start | bytes 3145736 | tf_op jit(solution)/shard_map/ppermute | solution.py:369
  298.1 43.2 %collective-permute-start.53 = (bf16[4,256,512]{2,1,0:T(8,128)(2,1)}, bf16[4,256,512]{2,1,0:T(8,128)(2,1)}, u32[]{:S(2)}, u32[]{:S(2)}) collective-permute-start(bf16[4,256,512]{2,1,0:T(8,128)(2,1)} %collective-permute-done.51), channel_id=1, source_target_pairs={{0,1},{1,2},{2,3},{3,0},{4,5},{5,6},{6,7},{7,4},{8,9},{9,10},{10,1... | collective-permute-start | bytes 3145736 | tf_op jit(solution)/shard_map/ppermute | solution.py:382
  309.1 46.2 %collective-permute-start.43 = (bf16[4,256,512]{2,1,0:T(8,128)(2,1)}, bf16[4,256,512]{2,1,0:T(8,128)(2,1)}, u32[]{:S(2)}, u32[]{:S(2)}) collective-permute-start(bf16[4,256,512]{2,1,0:T(8,128)(2,1)} %collective-permute-done.41), channel_id=1, source_target_pairs={{0,1},{1,2},{2,3},{3,0},{4,5},{5,6},{6,7},{7,4},{8,9},{9,10},{10,1... | collective-permute-start | bytes 3145736 | tf_op jit(solution)/shard_map/ppermute | solution.py:382
  311.9 44.6 %collective-permute-start.13 = (bf16[4,256,384]{1,2,0:T(8,128)(2,1)}, bf16[4,256,384]{1,2,0:T(8,128)(2,1)S(1)}, u32[]{:S(2)}, u32[]{:S(2)}) collective-permute-start(bf16[4,256,384]{1,2,0:T(8,128)(2,1)} %collective-permute-done.12), channel_id=1, source_target_pairs={{0,4},{4,0},{8,12},{12,8},{16,20},{20,16},{24,28},{28,24},{1,5},{5... | collective-permute-start | bytes 2359304 | tf_op jit(solution)/shard_map/ppermute | solution.py:373
  341.4 59.6 %collective-permute-start.63 = (bf16[4,256,512]{2,1,0:T(8,128)(2,1)}, bf16[4,256,512]{2,1,0:T(8,128)(2,1)}, u32[]{:S(2)}, u32[]{:S(2)}) collective-permute-start(bf16[4,256,512]{2,1,0:T(8,128)(2,1)} %collective-permute-done.61), channel_id=1, source_target_pairs={{0,1},{1,2},{2,3},{3,0},{4,5},{5,6},{6,7},{7,4},{8,9},{9,10},{10,1... | collective-permute-start | bytes 3145736 | tf_op jit(solution)/shard_map/ppermute | solution.py:382
  341.4 61.2 %collective-permute-start.54 = (bf16[4,256,512]{2,1,0:T(8,128)(2,1)}, bf16[4,256,512]{2,1,0:T(8,128)(2,1)}, u32[]{:S(2)}, u32[]{:S(2)}) collective-permute-start(bf16[4,256,512]{2,1,0:T(8,128)(2,1)} %collective-permute-done.53), channel_id=1, source_target_pairs={{0,4},{4,0},{8,12},{12,8},{16,20},{20,16},{24,28},{28,24},{1,5},{5... | collective-permute-start | bytes 3145736 | tf_op jit(solution)/shard_map/ppermute | solution.py:373
  355.4 51.4 %collective-permute-start.55 = (bf16[4,256,512]{2,1,0:T(8,128)(2,1)}, bf16[4,256,512]{2,1,0:T(8,128)(2,1)}, u32[]{:S(2)}, u32[]{:S(2)}) collective-permute-start(bf16[4,256,512]{2,1,0:T(8,128)(2,1)} %collective-permute-done.53), channel_id=1, source_target_pairs={{0,1},{1,2},{2,3},{3,0},{4,5},{5,6},{6,7},{7,4},{8,9},{9,10},{10,1... | collective-permute-start | bytes 3145736 | tf_op jit(solution)/shard_map/ppermute | solution.py:382
  355.4 49.2 %collective-permute-start.44 = (bf16[4,256,512]{2,1,0:T(8,128)(2,1)}, bf16[4,256,512]{2,1,0:T(8,128)(2,1)}, u32[]{:S(2)}, u32[]{:S(2)}) collective-permute-start(bf16[4,256,512]{2,1,0:T(8,128)(2,1)} %collective-permute-done.43), channel_id=1, source_target_pairs={{0,4},{4,0},{8,12},{12,8},{16,20},{20,16},{24,28},{28,24},{1,5},{5... | collective-permute-start | bytes 3145736 | tf_op jit(solution)/shard_map/ppermute | solution.py:373
  356.5 66.3 %collective-permute-start.45 = (bf16[4,256,512]{2,1,0:T(8,128)(2,1)}, bf16[4,256,512]{2,1,0:T(8,128)(2,1)}, u32[]{:S(2)}, u32[]{:S(2)}) collective-permute-start(bf16[4,256,512]{2,1,0:T(8,128)(2,1)} %collective-permute-done.43), channel_id=1, source_target_pairs={{0,1},{1,2},{2,3},{3,0},{4,5},{5,6},{6,7},{7,4},{8,9},{9,10},{10,1... | collective-permute-start | bytes 3145736 | tf_op jit(solution)/shard_map/ppermute | solution.py:382
  404.5 40.1 %collective-permute-start.65 = (bf16[4,256,512]{2,1,0:T(8,128)(2,1)}, bf16[4,256,512]{2,1,0:T(8,128)(2,1)S(1)}, u32[]{:S(2)}, u32[]{:S(2)}) collective-permute-start(bf16[4,256,512]{2,1,0:T(8,128)(2,1)} %collective-permute-done.63), channel_id=1, source_target_pairs={{0,1},{1,2},{2,3},{3,0},{4,5},{5,6},{6,7},{7,4},{8,9},{9,10},{10,1... | collective-permute-start | bytes 3145736 | tf_op jit(solution)/shard_map/ppermute | solution.py:382
  406.8 42.2 %collective-permute-start.29 = (bf16[256,2048]{1,0:T(8,128)(2,1)S(1)}, bf16[256,2048]{1,0:T(8,128)(2,1)S(1)}, u32[]{:S(2)}, u32[]{:S(2)}) collective-permute-start(bf16[256,2048]{1,0:T(8,128)(2,1)S(1)} %pad_maximum_fusion.28), channel_id=1, source_target_pairs={{0,8},{4,12},{8,0},{12,4},{16,24},{20,28},{24,16},{28,20},{1,9},{5... | collective-permute-start | bytes 3145736 | tf_op jit(solution)/shard_map/ppermute | solution.py:369
  427.0 44.2 %collective-permute-start.73 = (bf16[256,2048]{1,0:T(8,128)(2,1)S(1)}, bf16[256,2048]{1,0:T(8,128)(2,1)S(1)}, u32[]{:S(2)}, u32[]{:S(2)}) collective-permute-start(bf16[256,2048]{1,0:T(8,128)(2,1)S(1)} %pad_maximum_fusion.36), channel_id=1, source_target_pairs={{0,16},{4,20},{8,24},{12,28},{16,0},{20,4},{24,8},{28,12},{1,17},{... | collective-permute-start | bytes 3145736 | tf_op jit(solution)/shard_map/ppermute | solution.py:369
  428.7 52.1 %collective-permute-start.72 = (bf16[128,2048]{1,0:T(8,128)(2,1)S(1)}, bf16[128,2048]{1,0:T(8,128)(2,1)S(1)}, u32[]{:S(2)}, u32[]{:S(2)}) collective-permute-start(bf16[128,2048]{1,0:T(8,128)(2,1)S(1)} %add_convert_fusion.17), channel_id=1, source_target_pairs={{0,16},{4,20},{8,24},{12,28},{16,0},{20,4},{24,8},{28,12},{1,17},{... | collective-permute-start | bytes 1572872 | tf_op jit(solution)/shard_map/ppermute | solution.py:369
  444.7 39.0 %collective-permute-start.56 = (bf16[4,256,512]{2,1,0:T(8,128)(2,1)}, bf16[4,256,512]{2,1,0:T(8,128)(2,1)S(1)}, u32[]{:S(2)}, u32[]{:S(2)}) collective-permute-start(bf16[4,256,512]{2,1,0:T(8,128)(2,1)} %collective-permute-done.55), channel_id=1, source_target_pairs={{0,4},{4,0},{8,12},{12,8},{16,20},{20,16},{24,28},{28,24},{1,5},{5... | collective-permute-start | bytes 3145736 | tf_op jit(solution)/shard_map/ppermute | solution.py:373
  449.0 37.9 %collective-permute-start.46 = (bf16[4,256,512]{2,1,0:T(8,128)(2,1)}, bf16[4,256,512]{2,1,0:T(8,128)(2,1)S(1)}, u32[]{:S(2)}, u32[]{:S(2)}) collective-permute-start(bf16[4,256,512]{2,1,0:T(8,128)(2,1)} %collective-permute-done.45), channel_id=1, source_target_pairs={{0,4},{4,0},{8,12},{12,8},{16,20},{20,16},{24,28},{28,24},{1,5},{5... | collective-permute-start | bytes 3145736 | tf_op jit(solution)/shard_map/ppermute | solution.py:373
  449.0 64.4 %collective-permute-start.66 = (bf16[4,256,512]{2,1,0:T(8,128)(2,1)S(1)}, bf16[4,256,512]{2,1,0:T(8,128)(2,1)S(1)}, u32[]{:S(2)}, u32[]{:S(2)}) collective-permute-start(bf16[4,256,512]{2,1,0:T(8,128)(2,1)S(1)} %collective-permute-done.65), channel_id=1, source_target_pairs={{0,4},{4,0},{8,12},{12,8},{16,20},{20,16},{24,28},{28,24},{1,5},{5... | collective-permute-start | bytes 3145736 | tf_op jit(solution)/shard_map/ppermute | solution.py:373
  544.4 101.9 %collective-permute-start.76 = (bf16[256,2048]{1,0:T(8,128)(2,1)}, bf16[256,2048]{1,0:T(8,128)(2,1)}, u32[]{:S(2)}, u32[]{:S(2)}) collective-permute-start(bf16[256,2048]{1,0:T(8,128)(2,1)} %get-tuple-element.69), channel_id=1, source_target_pairs={{0,8},{4,12},{8,0},{12,4},{16,24},{20,28},{24,16},{28,20},{1,9},{5... | collective-permute-start | bytes 3145736 | tf_op jit(solution)/shard_map/ppermute | solution.py:369
  545.4 98.8 %collective-permute-start.77 = (bf16[256,2048]{1,0:T(8,128)(2,1)}, bf16[256,2048]{1,0:T(8,128)(2,1)}, u32[]{:S(2)}, u32[]{:S(2)}) collective-permute-start(bf16[256,2048]{1,0:T(8,128)(2,1)} %get-tuple-element.69), channel_id=1, source_target_pairs={{0,16},{4,20},{8,24},{12,28},{16,0},{20,4},{24,8},{28,12},{1,17},{... | collective-permute-start | bytes 3145736 | tf_op jit(solution)/shard_map/ppermute | solution.py:369
  640.8 186.8 %collective-permute-start.90 = (bf16[256,2048]{1,0:T(8,128)(2,1)}, bf16[256,2048]{1,0:T(8,128)(2,1)}, u32[]{:S(2)}, u32[]{:S(2)}) collective-permute-start(bf16[256,2048]{1,0:T(8,128)(2,1)} %pad_maximum_fusion.41), channel_id=1, source_target_pairs={{0,16},{4,20},{8,24},{12,28},{16,0},{20,4},{24,8},{28,12},{1,17},{... | collective-permute-start | bytes 3145736 | tf_op jit(solution)/shard_map/ppermute | solution.py:369
  644.2 189.0 %collective-permute-start.69 = (bf16[256,2048]{1,0:T(8,128)(2,1)}, bf16[256,2048]{1,0:T(8,128)(2,1)}, u32[]{:S(2)}, u32[]{:S(2)}) collective-permute-start(bf16[256,2048]{1,0:T(8,128)(2,1)} %pad_maximum_fusion.34), channel_id=1, source_target_pairs={{0,16},{4,20},{8,24},{12,28},{16,0},{20,4},{24,8},{28,12},{1,17},{... | collective-permute-start | bytes 3145736 | tf_op jit(solution)/shard_map/ppermute | solution.py:369
  650.7 50.0 %collective-permute-start.79 = (bf16[128,2048]{1,0:T(8,128)(2,1)S(1)}, bf16[128,2048]{1,0:T(8,128)(2,1)S(1)}, u32[]{:S(2)}, u32[]{:S(2)}) collective-permute-start(bf16[128,2048]{1,0:T(8,128)(2,1)S(1)} %slice.846), channel_id=1, source_target_pairs={{0,16},{4,20},{8,24},{12,28},{16,0},{20,4},{24,8},{28,12},{1,17},{... | collective-permute-start | bytes 1572872 | tf_op jit(solution)/shard_map/ppermute | solution.py:369
  672.9 155.8 %collective-permute-start.89 = (bf16[128,2048]{1,0:T(8,128)(2,1)}, bf16[128,2048]{1,0:T(8,128)(2,1)}, u32[]{:S(2)}, u32[]{:S(2)}) collective-permute-start(bf16[128,2048]{1,0:T(8,128)(2,1)} %add_convert_fusion.11), channel_id=1, source_target_pairs={{0,16},{4,20},{8,24},{12,28},{16,0},{20,4},{24,8},{28,12},{1,17},{... | collective-permute-start | bytes 1572872 | tf_op jit(solution)/shard_map/ppermute | solution.py:369
  679.9 153.2 %collective-permute-start.68 = (bf16[128,2048]{1,0:T(8,128)(2,1)}, bf16[128,2048]{1,0:T(8,128)(2,1)}, u32[]{:S(2)}, u32[]{:S(2)}) collective-permute-start(bf16[128,2048]{1,0:T(8,128)(2,1)} %add_convert_fusion.19), channel_id=1, source_target_pairs={{0,16},{4,20},{8,24},{12,28},{16,0},{20,4},{24,8},{28,12},{1,17},{... | collective-permute-start | bytes 1572872 | tf_op jit(solution)/shard_map/ppermute | solution.py:369
  825.5 68.0 %collective-permute-start.102 = (bf16[256,2048]{1,0:T(8,128)(2,1)}, bf16[256,2048]{1,0:T(8,128)(2,1)}, u32[]{:S(2)}, u32[]{:S(2)}) collective-permute-start(bf16[256,2048]{1,0:T(8,128)(2,1)} %pad_maximum_fusion.43), channel_id=1, source_target_pairs={{0,16},{4,20},{8,24},{12,28},{16,0},{20,4},{24,8},{28,12},{1,17},{... | collective-permute-start | bytes 3145736 | tf_op jit(solution)/shard_map/ppermute | solution.py:369
  827.6 53.6 %collective-permute-start.100 = (bf16[256,2048]{1,0:T(8,128)(2,1)}, bf16[256,2048]{1,0:T(8,128)(2,1)}, u32[]{:S(2)}, u32[]{:S(2)}) collective-permute-start(bf16[256,2048]{1,0:T(8,128)(2,1)} %pad_maximum_fusion.42), channel_id=1, source_target_pairs={{0,8},{4,12},{8,0},{12,4},{16,24},{20,28},{24,16},{28,20},{1,9},{5... | collective-permute-start | bytes 3145736 | tf_op jit(solution)/shard_map/ppermute | solution.py:369
  832.1 44.4 %collective-permute-start.91 = (bf16[128,2048]{1,0:T(8,128)(2,1)}, bf16[128,2048]{1,0:T(8,128)(2,1)}, u32[]{:S(2)}, u32[]{:S(2)}) collective-permute-start(bf16[128,2048]{1,0:T(8,128)(2,1)} %get-tuple-element.135), channel_id=1, source_target_pairs={{0,8},{4,12},{8,0},{12,4},{16,24},{20,28},{24,16},{28,20},{1,9},{5... | collective-permute-start | bytes 1572872 | tf_op jit(solution)/shard_map/ppermute | solution.py:369
  836.3 46.6 %collective-permute-start.70 = (bf16[128,2048]{1,0:T(8,128)(2,1)}, bf16[128,2048]{1,0:T(8,128)(2,1)S(1)}, u32[]{:S(2)}, u32[]{:S(2)}) collective-permute-start(bf16[128,2048]{1,0:T(8,128)(2,1)} %get-tuple-element.153), channel_id=1, source_target_pairs={{0,8},{4,12},{8,0},{12,4},{16,24},{20,28},{24,16},{28,20},{1,9},{5... | collective-permute-start | bytes 1572872 | tf_op jit(solution)/shard_map/ppermute | solution.py:369
  849.3 51.1 %collective-permute-start.82 = (bf16[256,2048]{1,0:T(8,128)(2,1)S(1)}, bf16[256,2048]{1,0:T(8,128)(2,1)S(1)}, u32[]{:S(2)}, u32[]{:S(2)}) collective-permute-start(bf16[256,2048]{1,0:T(8,128)(2,1)S(1)} %pad_maximum_fusion.39), channel_id=1, source_target_pairs={{0,16},{4,20},{8,24},{12,28},{16,0},{20,4},{24,8},{28,12},{1,17},{... | collective-permute-start | bytes 3145736 | tf_op jit(solution)/shard_map/ppermute | solution.py:369
  881.2 119.8 %collective-permute-start.146 = (bf16[4,256,2048]{2,1,0:T(8,128)(2,1)}, bf16[4,256,2048]{2,1,0:T(8,128)(2,1)}, u32[]{:S(2)}, u32[]{:S(2)}) collective-permute-start(bf16[4,256,2048]{2,1,0:T(8,128)(2,1)} %fusion.18), channel_id=1, source_target_pairs={{0,4},{4,0},{8,12},{12,8},{16,20},{20,16},{24,28},{28,24},{1,5},{5... | collective-permute-start | bytes 12582920 | tf_op jit(solution)/shard_map/ppermute | solution.py:373
  942.4 70.7 %collective-permute-start.132 = (bf16[4,256,2048]{2,1,0:T(8,128)(2,1)}, bf16[4,256,2048]{2,1,0:T(8,128)(2,1)}, u32[]{:S(2)}, u32[]{:S(2)}) collective-permute-start(bf16[4,256,2048]{2,1,0:T(8,128)(2,1)} %fusion.16), channel_id=1, source_target_pairs={{0,4},{4,0},{8,12},{12,8},{16,20},{20,16},{24,28},{28,24},{1,5},{5... | collective-permute-start | bytes 12582920 | tf_op jit(solution)/shard_map/ppermute | solution.py:373
  953.6 72.0 %collective-permute-start.139 = (bf16[4,256,2048]{2,1,0:T(8,128)(2,1)}, bf16[4,256,2048]{2,1,0:T(8,128)(2,1)}, u32[]{:S(2)}, u32[]{:S(2)}) collective-permute-start(bf16[4,256,2048]{2,1,0:T(8,128)(2,1)} %fusion.17), channel_id=1, source_target_pairs={{0,4},{4,0},{8,12},{12,8},{16,20},{20,16},{24,28},{28,24},{1,5},{5... | collective-permute-start | bytes 12582920 | tf_op jit(solution)/shard_map/ppermute | solution.py:373
  994.6 37.0 %collective-permute-start.107 = (bf16[128,2048]{1,0:T(8,128)(2,1)}, bf16[128,2048]{1,0:T(8,128)(2,1)}, u32[]{:S(2)}, u32[]{:S(2)}) collective-permute-start(bf16[128,2048]{1,0:T(8,128)(2,1)} %slice.889), channel_id=1, source_target_pairs={{0,8},{4,12},{8,0},{12,4},{16,24},{20,28},{24,16},{28,20},{1,9},{5... | collective-permute-start | bytes 1572872 | tf_op jit(solution)/shard_map/ppermute | solution.py:369
  996.5 37.6 %collective-permute-start.108 = (bf16[128,2048]{1,0:T(8,128)(2,1)}, bf16[128,2048]{1,0:T(8,128)(2,1)}, u32[]{:S(2)}, u32[]{:S(2)}) collective-permute-start(bf16[128,2048]{1,0:T(8,128)(2,1)} %slice.890), channel_id=1, source_target_pairs={{0,16},{4,20},{8,24},{12,28},{16,0},{20,4},{24,8},{28,12},{1,17},{... | collective-permute-start | bytes 1572872 | tf_op jit(solution)/shard_map/ppermute | solution.py:369
  1010.8 126.6 %collective-permute-start.147 = (bf16[4,256,512]{2,1,0:T(8,128)(2,1)}, bf16[4,256,512]{2,1,0:T(8,128)(2,1)}, u32[]{:S(2)}, u32[]{:S(2)}) collective-permute-start(bf16[4,256,512]{2,1,0:T(8,128)(2,1)} %slice.1127), channel_id=1, source_target_pairs={{0,3},{1,0},{2,1},{3,2},{4,7},{5,4},{6,5},{7,6},{8,11},{9,8},{10,9... | collective-permute-start | bytes 3145736 | tf_op jit(solution)/shard_map/ppermute | solution.py:387
  1023.1 116.3 %collective-permute-start.133 = (bf16[4,256,512]{2,1,0:T(8,128)(2,1)}, bf16[4,256,512]{2,1,0:T(8,128)(2,1)}, u32[]{:S(2)}, u32[]{:S(2)}) collective-permute-start(bf16[4,256,512]{2,1,0:T(8,128)(2,1)} %slice.1129), channel_id=1, source_target_pairs={{0,3},{1,0},{2,1},{3,2},{4,7},{5,4},{6,5},{7,6},{8,11},{9,8},{10,9... | collective-permute-start | bytes 3145736 | tf_op jit(solution)/shard_map/ppermute | solution.py:387
  1031.6 115.6 %collective-permute-start.140 = (bf16[4,256,512]{2,1,0:T(8,128)(2,1)}, bf16[4,256,512]{2,1,0:T(8,128)(2,1)}, u32[]{:S(2)}, u32[]{:S(2)}) collective-permute-start(bf16[4,256,512]{2,1,0:T(8,128)(2,1)} %slice.1128), channel_id=1, source_target_pairs={{0,3},{1,0},{2,1},{3,2},{4,7},{5,4},{6,5},{7,6},{8,11},{9,8},{10,9... | collective-permute-start | bytes 3145736 | tf_op jit(solution)/shard_map/ppermute | solution.py:387
  1087.9 69.6 %collective-permute-start.111 = (bf16[256,2048]{1,0:T(8,128)(2,1)}, bf16[256,2048]{1,0:T(8,128)(2,1)}, u32[]{:S(2)}, u32[]{:S(2)}) collective-permute-start(bf16[256,2048]{1,0:T(8,128)(2,1)} %pad_maximum_fusion.45), channel_id=1, source_target_pairs={{0,16},{4,20},{8,24},{12,28},{16,0},{20,4},{24,8},{28,12},{1,17},{... | collective-permute-start | bytes 3145736 | tf_op jit(solution)/shard_map/ppermute | solution.py:369
  1090.0 52.1 %collective-permute-start.109 = (bf16[256,2048]{1,0:T(8,128)(2,1)}, bf16[256,2048]{1,0:T(8,128)(2,1)}, u32[]{:S(2)}, u32[]{:S(2)}) collective-permute-start(bf16[256,2048]{1,0:T(8,128)(2,1)} %pad_maximum_fusion.44), channel_id=1, source_target_pairs={{0,8},{4,12},{8,0},{12,4},{16,24},{20,28},{24,16},{28,20},{1,9},{5... | collective-permute-start | bytes 3145736 | tf_op jit(solution)/shard_map/ppermute | solution.py:369
  1155.2 75.7 %collective-permute-start.148 = (bf16[4,256,512]{2,1,0:T(8,128)(2,1)S(1)}, bf16[4,256,512]{2,1,0:T(8,128)(2,1)S(1)}, u32[]{:S(2)}, u32[]{:S(2)}) collective-permute-start(bf16[4,256,512]{2,1,0:T(8,128)(2,1)S(1)} %fusion.42), channel_id=1, source_target_pairs={{0,3},{1,0},{2,1},{3,2},{4,7},{5,4},{6,5},{7,6},{8,11},{9,8},{10,9... | collective-permute-start | bytes 3145736 | tf_op jit(solution)/shard_map/ppermute | solution.py:387
  1157.5 220.4 %collective-permute-start.118 = (bf16[4,256,1536]{2,1,0:T(8,128)(2,1)}, bf16[4,256,1536]{2,1,0:T(8,128)(2,1)}, u32[]{:S(2)}, u32[]{:S(2)}) collective-permute-start(bf16[4,256,1536]{2,1,0:T(8,128)(2,1)} %fusion.19), channel_id=1, source_target_pairs={{0,4},{4,0},{8,12},{12,8},{16,20},{20,16},{24,28},{28,24},{1,5},{5... | collective-permute-start | bytes 9437192 | tf_op jit(solution)/shard_map/ppermute | solution.py:373
  1164.9 67.4 %collective-permute-start.134 = (bf16[4,256,512]{2,1,0:T(8,128)(2,1)S(1)}, bf16[4,256,512]{2,1,0:T(8,128)(2,1)S(1)}, u32[]{:S(2)}, u32[]{:S(2)}) collective-permute-start(bf16[4,256,512]{2,1,0:T(8,128)(2,1)S(1)} %fusion.46), channel_id=1, source_target_pairs={{0,3},{1,0},{2,1},{3,2},{4,7},{5,4},{6,5},{7,6},{8,11},{9,8},{10,9... | collective-permute-start | bytes 3145736 | tf_op jit(solution)/shard_map/ppermute | solution.py:387
  1168.2 65.7 %collective-permute-start.141 = (bf16[4,256,512]{2,1,0:T(8,128)(2,1)S(1)}, bf16[4,256,512]{2,1,0:T(8,128)(2,1)S(1)}, u32[]{:S(2)}, u32[]{:S(2)}) collective-permute-start(bf16[4,256,512]{2,1,0:T(8,128)(2,1)S(1)} %fusion.44), channel_id=1, source_target_pairs={{0,3},{1,0},{2,1},{3,2},{4,7},{5,4},{6,5},{7,6},{8,11},{9,8},{10,9... | collective-permute-start | bytes 3145736 | tf_op jit(solution)/shard_map/ppermute | solution.py:387
  1178.5 51.2 %collective-permute-start.127 = (bf16[4,256,128]{2,1,0:T(8,128)(2,1)S(1)}, bf16[4,256,128]{2,1,0:T(8,128)(2,1)S(1)}, u32[]{:S(2)}, u32[]{:S(2)}) collective-permute-start(bf16[4,256,128]{2,1,0:T(8,128)(2,1)S(1)} %fusion.56), channel_id=1, source_target_pairs={{0,3},{1,0},{2,1},{3,2},{4,7},{5,4},{6,5},{7,6},{8,11},{9,8},{10,9... | collective-permute-start | bytes 786440 | tf_op jit(solution)/shard_map/ppermute | solution.py:387
  1229.8 39.1 %collective-permute-start.112 = (bf16[128,2048]{1,0:T(8,128)(2,1)S(1)}, bf16[128,2048]{1,0:T(8,128)(2,1)S(1)}, u32[]{:S(2)}, u32[]{:S(2)}) collective-permute-start(bf16[128,2048]{1,0:T(8,128)(2,1)S(1)} %get-tuple-element.107), channel_id=1, source_target_pairs={{0,8},{4,12},{8,0},{12,4},{16,24},{20,28},{24,16},{28,20},{1,9},{5... | collective-permute-start | bytes 1572872 | tf_op jit(solution)/shard_map/ppermute | solution.py:369
  1231.0 37.9 %collective-permute-start.114 = (bf16[128,2048]{1,0:T(8,128)(2,1)S(1)}, bf16[128,2048]{1,0:T(8,128)(2,1)S(1)}, u32[]{:S(2)}, u32[]{:S(2)}) collective-permute-start(bf16[128,2048]{1,0:T(8,128)(2,1)S(1)} %get-tuple-element.106), channel_id=1, source_target_pairs={{0,16},{4,20},{8,24},{12,28},{16,0},{20,4},{24,8},{28,12},{1,17},{... | collective-permute-start | bytes 1572872 | tf_op jit(solution)/shard_map/ppermute | solution.py:369
  1232.3 37.5 %collective-permute-start.116 = (bf16[128,2048]{1,0:T(8,128)(2,1)S(1)}, bf16[128,2048]{1,0:T(8,128)(2,1)S(1)}, u32[]{:S(2)}, u32[]{:S(2)}) collective-permute-start(bf16[128,2048]{1,0:T(8,128)(2,1)S(1)} %get-tuple-element.105), channel_id=1, source_target_pairs={{0,8},{4,12},{8,0},{12,4},{16,24},{20,28},{24,16},{28,20},{1,9},{5... | collective-permute-start | bytes 1572872 | tf_op jit(solution)/shard_map/ppermute | solution.py:369
  1268.9 45.2 %collective-permute-start.135 = (bf16[4,256,512]{2,1,0:T(8,128)(2,1)S(1)}, bf16[4,256,512]{2,1,0:T(8,128)(2,1)S(1)}, u32[]{:S(2)}, u32[]{:S(2)}) collective-permute-start(bf16[4,256,512]{2,1,0:T(8,128)(2,1)S(1)} %fusion.47), channel_id=1, source_target_pairs={{0,3},{1,0},{2,1},{3,2},{4,7},{5,4},{6,5},{7,6},{8,11},{9,8},{10,9... | collective-permute-start | bytes 3145736 | tf_op jit(solution)/shard_map/ppermute | solution.py:387
  1268.9 67.7 %collective-permute-start.142 = (bf16[4,256,512]{2,1,0:T(8,128)(2,1)S(1)}, bf16[4,256,512]{2,1,0:T(8,128)(2,1)S(1)}, u32[]{:S(2)}, u32[]{:S(2)}) collective-permute-start(bf16[4,256,512]{2,1,0:T(8,128)(2,1)S(1)} %fusion.45), channel_id=1, source_target_pairs={{0,3},{1,0},{2,1},{3,2},{4,7},{5,4},{6,5},{7,6},{8,11},{9,8},{10,9... | collective-permute-start | bytes 3145736 | tf_op jit(solution)/shard_map/ppermute | solution.py:387
  1272.2 114.2 %collective-permute-start.117 = (bf16[256,2048]{1,0:T(8,128)(2,1)S(1)}, bf16[256,2048]{1,0:T(8,128)(2,1)S(1)}, u32[]{:S(2)}, u32[]{:S(2)}) collective-permute-start(bf16[256,2048]{1,0:T(8,128)(2,1)S(1)} %pad_maximum_fusion.48), channel_id=1, source_target_pairs={{0,1},{1,0},{2,3},{3,2},{4,5},{5,4},{6,7},{7,6},{8,9},{9,8},{10,11... | collective-permute-start | bytes 3145736 | tf_op jit(solution)/shard_map/ppermute | solution.py:377
  1292.2 84.2 %collective-permute-start.150 = (bf16[256,512]{1,0:T(8,128)(2,1)S(1)}, bf16[256,512]{1,0:T(8,128)(2,1)S(1)}, u32[]{:S(2)}, u32[]{:S(2)}) collective-permute-start(bf16[256,512]{1,0:T(8,128)(2,1)S(1)} %get-tuple-element.160), channel_id=1, source_target_pairs={{0,8},{4,12},{8,0},{12,4},{16,24},{20,28},{24,16},{28,20},{1,9},{5... | collective-permute-start | bytes 786440 | tf_op jit(solution)/shard_map/ppermute | solution.py:369
  (242 other events, 3845.6 us)
